TPU v7x, 128 devices: a whole 4x4x4 slice. The times are simulated.
128 devices in a mesh: section: 2 (over z_hi), expert: 8 (over y, z_lo), dp: 8 (over x, core).
Axes of the slice: x: 4, y: 4, z: 4 (z_hi: 2, z_lo: 2; z = z_hi * 2 + z_lo), core: 2. Of those that a mesh axis runs over, the one named last changes fastest.
Arguments:
- inputs: bfloat16 [2, 512, 3072], P(None, ('expert', 'dp')), may hold values from -6 to 6
- cotangent: bfloat16 [2, 512, 3072], P(None, ('expert', 'dp')), may hold values from -6 to 6
- norm_gain: bfloat16 [2, 3072], P('section'), may hold values from 0.5 to 1.5
- router: bfloat16 [2, 3072, 8], P('section'), may hold values from -0.109375 to 0.109375
- w_gate: bfloat16 [2, 8, 3072, 8192], P('section', 'expert', None, 'dp'), may hold values from -0.109375 to 0.109375
- w_up: bfloat16 [2, 8, 3072, 8192], P('section', 'expert', None, 'dp'), may hold values from -0.109375 to 0.109375
- w_down: bfloat16 [2, 8, 8192, 3072], P('section', 'expert', 'dp'), may hold values from -0.0625 to 0.0625
- routes: int32 [2, 2, 512, 2], P('section', None, ('expert', 'dp')), may hold values from 0 to 7, as said below
Outputs:
- acts: bfloat16 [2, 2, 512, 3072], P('section', None, ('expert', 'dp'))
- grads: bfloat16 [2, 2, 512, 3072], P('section', None, ('expert', 'dp'))
- router_grad: float32 [2, 3072, 8], P('section')
Inputs may be any that keep to these rules, and one draw needn't show every extreme that they name: `routes`: the two experts of a token differ. For each layer and micro-batch, the 8 tokens of one device name no expert more than 3 times, and one expert, the same on all devices for that layer and micro-batch, exactly 3 times.
All inputs are finite; a program needn't handle non-finite values.
Results may differ from a plain program's by a relative error of at most 0.017.
Values may be sent and summed in bfloat16 or wider, within the bound.
A program may use at most 128 MiB of HBM per device.

v0:
```python
import jax
import jax.numpy as jnp
from jax import lax
from jax.sharding import PartitionSpec as P

EPSILON = 1e-05


def passed_along(block, axis, distance):
    devices = range(lax.axis_size(axis))
    route = [(i - distance, i) for i in devices if i - distance in devices]
    return lax.ppermute(block, axis, route)


def norm_rows(layer_in, gain_row):
    values = layer_in.astype(jnp.float32)
    inv_rms = lax.rsqrt(jnp.mean(values * values, axis=-1, keepdims=True) + EPSILON)
    return (values, inv_rms, (values * inv_rms * gain_row).astype(jnp.bfloat16))


def gate_probs(hidden, router_w, picks):
    logits = jnp.dot(hidden, router_w, preferred_element_type=jnp.float32)
    chosen = jnp.take_along_axis(logits, picks, axis=1)
    logit_gap = chosen[:, 0] - chosen[:, 1]
    return jnp.stack([jax.nn.sigmoid(logit_gap), jax.nn.sigmoid(-logit_gap)], axis=1)


def slot_table(picks, experts, capacity):
    flat_pick = picks.reshape(-1)
    onehot = (flat_pick[:, None] == jnp.arange(experts, dtype=jnp.int32)[None, :]).astype(jnp.int32)
    earlier = jnp.cumsum(onehot, axis=0) - onehot
    slot_pos = jnp.sum(earlier * onehot, axis=1)
    target = flat_pick * capacity + slot_pos
    return target[:, None] == jnp.arange(experts * capacity, dtype=jnp.int32)[None, :]


def deliver(outgoing, experts, capacity):
    model_width = outgoing.shape[1]
    grouped = outgoing.reshape(experts, capacity, model_width)
    tiled = jnp.repeat(grouped, lax.axis_size("dp"), axis=0)
    arrived = lax.all_to_all(tiled, ("expert", "dp"), split_axis=0, concat_axis=0, tiled=True)
    return arrived.reshape(-1, model_width)


def collect(partial_out, experts, capacity):
    model_width = partial_out.shape[1]
    replicas = lax.axis_size("dp")
    returned = lax.all_to_all(
        partial_out.reshape(experts * replicas, capacity, model_width),
        ("expert", "dp"),
        split_axis=0,
        concat_axis=0,
        tiled=True,
    )
    summed = jnp.sum(
        returned.reshape(experts, replicas, capacity, model_width).astype(jnp.float32), axis=1
    )
    return summed.reshape(experts * capacity, model_width)


def send_rows(placing, row_values):
    grouped = lax.dot_general(
        placing.astype(jnp.bfloat16),
        row_values,
        (((0,), (0,)), ((), ())),
        preferred_element_type=jnp.float32,
    )
    return grouped.astype(jnp.bfloat16)


def forward_layer(layer_in, picks, gain_row, router_w, gate_w, up_w, down_w, experts, capacity):
    values, inv_rms, hidden = norm_rows(layer_in, gain_row)
    gate_prob = gate_probs(hidden, router_w, picks)
    placing = slot_table(picks, experts, capacity)
    arrived = deliver(
        send_rows(placing, jnp.repeat(hidden, picks.shape[1], axis=0)), experts, capacity
    )
    gate_pre = jnp.dot(arrived, gate_w, preferred_element_type=jnp.float32)
    up_pre = jnp.dot(arrived, up_w, preferred_element_type=jnp.float32)
    active = (gate_pre * jax.nn.sigmoid(gate_pre) * up_pre).astype(jnp.bfloat16)
    partial_out = jnp.dot(active, down_w, preferred_element_type=jnp.float32).astype(jnp.bfloat16)
    summed = collect(partial_out, experts, capacity)
    picked = jnp.dot(placing.astype(jnp.float32), summed, precision=lax.Precision.HIGHEST)
    picked = picked.reshape(layer_in.shape[0], picks.shape[1], -1)
    layer_out = (values + jnp.sum(gate_prob[:, :, None] * picked, axis=1)).astype(jnp.bfloat16)
    return (layer_out, picked, gate_pre, up_pre)


def backward_layer(
    layer_in,
    upstream,
    picks,
    gain_row,
    router_w,
    gate_w,
    up_w,
    down_w,
    picked,
    gate_pre,
    up_pre,
    experts,
    capacity,
):
    values, inv_rms, hidden = norm_rows(layer_in, gain_row)
    gate_prob = gate_probs(hidden, router_w, picks)
    placing = slot_table(picks, experts, capacity)
    grad_out = upstream.astype(jnp.float32)
    d_prob = jnp.sum(grad_out[:, None, :] * picked, axis=2)
    d_gap = gate_prob[:, 0] * gate_prob[:, 1] * (d_prob[:, 0] - d_prob[:, 1])
    d_chosen = jnp.stack([d_gap, -d_gap], axis=1)
    expert_hot = (picks[:, :, None] == jnp.arange(experts, dtype=jnp.int32)[None, None, :]).astype(
        jnp.float32
    )
    d_logits = jnp.sum(d_chosen[:, :, None] * expert_hot, axis=1)
    scaled = (gate_prob[:, :, None] * grad_out[:, None, :]).astype(jnp.bfloat16)
    scaled = scaled.reshape(-1, grad_out.shape[1])
    arrived = deliver(send_rows(placing, scaled), experts, capacity)
    contract_last = (((1,), (1,)), ((), ()))
    d_active = lax.dot_general(arrived, down_w, contract_last, preferred_element_type=jnp.float32)
    gate_sig = jax.nn.sigmoid(gate_pre)
    d_gate = (d_active * up_pre * gate_sig * (1.0 + gate_pre * (1.0 - gate_sig))).astype(
        jnp.bfloat16
    )
    d_up = (d_active * gate_pre * gate_sig).astype(jnp.bfloat16)
    d_rows = lax.dot_general(d_gate, gate_w, contract_last, preferred_element_type=jnp.float32)
    d_rows = d_rows + lax.dot_general(d_up, up_w, contract_last, preferred_element_type=jnp.float32)
    summed = collect(d_rows.astype(jnp.bfloat16), experts, capacity)
    returned = jnp.dot(placing.astype(jnp.float32), summed, precision=lax.Precision.HIGHEST)
    returned = returned.reshape(layer_in.shape[0], picks.shape[1], -1)
    d_hidden = jnp.sum(returned, axis=1) + jnp.dot(
        d_logits, router_w.astype(jnp.float32).T, precision=lax.Precision.HIGHEST
    )
    router_term = jnp.dot(hidden.astype(jnp.float32).T, d_logits, precision=lax.Precision.HIGHEST)
    weighted = gain_row * d_hidden
    cubed = inv_rms * inv_rms * inv_rms
    d_in = (
        grad_out
        + inv_rms * weighted
        - values * cubed * jnp.mean(values * weighted, axis=-1, keepdims=True)
    )
    return (d_in.astype(jnp.bfloat16), router_term)


def fetch_micro(stored, which_mb):
    return lax.dynamic_index_in_dim(stored, which_mb, 0, keepdims=False)


def store_micro(stored, fresh, which_mb, in_range):
    previous = lax.dynamic_index_in_dim(stored, which_mb, 0, keepdims=False)
    return lax.dynamic_update_index_in_dim(
        stored, jnp.where(in_range, fresh, previous), which_mb, 0
    )


def per_device(inputs, cotangent, norm_gain, router, w_gate, w_up, w_down, routes):
    section_count = lax.axis_size("section")
    section_id = lax.axis_index("section")
    micro_count, tok_rows, model_width = inputs.shape
    experts = router.shape[2]
    top_k = routes.shape[3]
    capacity = 3 * top_k * tok_rows // (2 * experts)
    gate_w = w_gate[0, 0]
    up_w = w_up[0, 0]
    down_w = w_down[0, 0]
    gain_row = norm_gain[0].astype(jnp.float32)
    router_w = router[0]
    picks_all = routes[0]
    expert_rows = experts * lax.axis_size("dp") * capacity
    hidden_units = gate_w.shape[1]
    tick_count = micro_count + section_count - 1
    carried = jnp.zeros((tok_rows, model_width), jnp.bfloat16)
    outputs_all = jnp.zeros((micro_count, tok_rows, model_width), jnp.bfloat16)
    stash_in = jnp.zeros((micro_count, tok_rows, model_width), jnp.bfloat16)
    stash_pick = jnp.zeros((micro_count, tok_rows, top_k, model_width), jnp.float32)
    stash_gate = jnp.zeros((micro_count, expert_rows, hidden_units), jnp.float32)
    stash_up = jnp.zeros((micro_count, expert_rows, hidden_units), jnp.float32)
    for moment in range(tick_count):
        position = moment - section_id
        in_range = (position >= 0) & (position < micro_count)
        which_mb = jnp.clip(position, 0, micro_count - 1)
        layer_in = jnp.where(section_id == 0, fetch_micro(inputs, which_mb), carried)
        picks = fetch_micro(picks_all, which_mb)
        layer_out, picked, gate_pre, up_pre = forward_layer(
            layer_in, picks, gain_row, router_w, gate_w, up_w, down_w, experts, capacity
        )
        outputs_all = store_micro(outputs_all, layer_out, which_mb, in_range)
        stash_in = store_micro(stash_in, layer_in, which_mb, in_range)
        stash_pick = store_micro(stash_pick, picked, which_mb, in_range)
        stash_gate = store_micro(stash_gate, gate_pre, which_mb, in_range)
        stash_up = store_micro(stash_up, up_pre, which_mb, in_range)
        if moment + 1 < tick_count:
            carried = passed_along(layer_out, "section", 1)
    carried = jnp.zeros((tok_rows, model_width), jnp.bfloat16)
    grads_all = jnp.zeros((micro_count, tok_rows, model_width), jnp.bfloat16)
    router_sum = jnp.zeros((model_width, experts), jnp.float32)
    for moment in range(tick_count):
        position = moment - (section_count - 1 - section_id)
        in_range = (position >= 0) & (position < micro_count)
        which_mb = jnp.clip(position, 0, micro_count - 1)
        upstream = jnp.where(
            section_id == section_count - 1, fetch_micro(cotangent, which_mb), carried
        )
        d_in, router_term = backward_layer(
            fetch_micro(stash_in, which_mb),
            upstream,
            fetch_micro(picks_all, which_mb),
            gain_row,
            router_w,
            gate_w,
            up_w,
            down_w,
            fetch_micro(stash_pick, which_mb),
            fetch_micro(stash_gate, which_mb),
            fetch_micro(stash_up, which_mb),
            experts,
            capacity,
        )
        grads_all = store_micro(grads_all, d_in, which_mb, in_range)
        router_sum = router_sum + jnp.where(in_range, router_term, 0.0)
        if moment + 1 < tick_count:
            carried = passed_along(d_in, "section", -1)
    router_total = lax.psum(router_sum, ("expert", "dp"))
    return (outputs_all[None], grads_all[None], router_total[None])


def solution(mesh):
    placed = (
        P(None, ("expert", "dp"), None),
        P(None, ("expert", "dp"), None),
        P("section", None),
        P("section", None, None),
        P("section", "expert", None, "dp"),
        P("section", "expert", None, "dp"),
        P("section", "expert", "dp", None),
        P("section", None, ("expert", "dp"), None),
    )
    return jax.shard_map(
        per_device,
        mesh=mesh,
        in_specs=placed,
        out_specs=(
            P("section", None, ("expert", "dp"), None),
            P("section", None, ("expert", "dp"), None),
            P("section", None, None),
        ),
        check_vma=False,
    )
```

profile of v0, /device:TPU:1, one launch (start us, length us, event | category | flops | bytes accessed | tf_op | source)
XLA Modules:
  0.0 984.1 jit_solution(17254181758903616295)
XLA Ops:
  13.8 10.5 %all-to-all-start = ((bf16[64,3,3072]{2,1,0:T(4,128)(2,1)}), bf16[64,3,3072]{2,1,0:T(4,128)(2,1)S(1)}, u32[]{:S(2)}, u32[]{:S(2)}) async-start(bf16[64,3,3072]{2,1,0:T(4,128)(2,1)} %bitcast.7), calls=%async_computation | async-start | bytes 3145728 | tf_op jit(solution)/shard_map/all_to_all | solution.py:41
  31.6 16.1 %all-to-all-done = bf16[64,3,3072]{2,1,0:T(4,128)(2,1)S(1)} async-done(((bf16[64,3,3072]{2,1,0:T(4,128)(2,1)}), bf16[64,3,3072]{2,1,0:T(4,128)(2,1)S(1)}, u32[]{:S(2)}, u32[]{:S(2)}) %all-to-all-start) | async-done | bytes 1179680 | tf_op jit(solution)/shard_map/all_to_all | solution.py:41
  62.3 5.0 all-to-all-start.1
  72.6 18.2 %all-to-all-done.1 = bf16[64,3,3072]{2,1,0:T(4,128)(2,1)S(1)} async-done(((bf16[64,3,3072]{2,1,0:T(4,128)(2,1)}), bf16[64,3,3072]{2,1,0:T(4,128)(2,1)S(1)}, u32[]{:S(2)}, u32[]{:S(2)}) %all-to-all-start.1) | async-done | bytes 1179680 | tf_op jit(solution)/shard_map/all_to_all | solution.py:48
  93.7 5.2 collective-permute-start
  105.1 5.9 all-to-all-start.2
  114.0 20.4 %all-to-all-done.2 = bf16[64,3,3072]{2,1,0:T(4,128)(2,1)} async-done(((bf16[64,3,3072]{2,1,0:T(4,128)(2,1)}), bf16[64,3,3072]{2,1,0:T(4,128)(2,1)}, u32[]{:S(2)}, u32[]{:S(2)}) %all-to-all-start.2) | async-done | bytes 1179680 | tf_op jit(solution)/shard_map/all_to_all | solution.py:41
  137.4 5.4 bitcast_dynamic-update-slice_fusion.4
  149.0 5.0 all-to-all-start.3
  156.5 21.0 %all-to-all-done.3 = bf16[64,3,3072]{2,1,0:T(4,128)(2,1)S(1)} async-done(((bf16[64,3,3072]{2,1,0:T(4,128)(2,1)}), bf16[64,3,3072]{2,1,0:T(4,128)(2,1)S(1)}, u32[]{:S(2)}, u32[]{:S(2)}) %all-to-all-start.3) | async-done | bytes 1179680 | tf_op jit(solution)/shard_map/all_to_all | solution.py:48
  189.6 6.8 all-to-all-start.4
  198.9 21.0 %all-to-all-done.4 = bf16[64,3,3072]{2,1,0:T(4,128)(2,1)} async-done(((bf16[64,3,3072]{2,1,0:T(4,128)(2,1)}), bf16[64,3,3072]{2,1,0:T(4,128)(2,1)}, u32[]{:S(2)}, u32[]{:S(2)}) %all-to-all-start.4) | async-done | bytes 1179680 | tf_op jit(solution)/shard_map/all_to_all | solution.py:41
  222.8 5.4 bitcast_dynamic-update-slice_fusion.3
  234.4 4.9 all-to-all-start.5
  241.2 21.5 %all-to-all-done.5 = bf16[64,3,3072]{2,1,0:T(4,128)(2,1)S(1)} async-done(((bf16[64,3,3072]{2,1,0:T(4,128)(2,1)}), bf16[64,3,3072]{2,1,0:T(4,128)(2,1)S(1)}, u32[]{:S(2)}, u32[]{:S(2)}) %all-to-all-start.5) | async-done | bytes 1179680 | tf_op jit(solution)/shard_map/all_to_all | solution.py:48
  268.0 5.8 all-to-all-start.6
  276.0 21.1 %all-to-all-done.6 = bf16[64,3,3072]{2,1,0:T(4,128)(2,1)} async-done(((bf16[64,3,3072]{2,1,0:T(4,128)(2,1)}), bf16[64,3,3072]{2,1,0:T(4,128)(2,1)}, u32[]{:S(2)}, u32[]{:S(2)}) %all-to-all-start.6) | async-done | bytes 1179680 | tf_op jit(solution)/shard_map/all_to_all | solution.py:41
  300.0 5.1 fusion.4
  313.3 4.9 all-to-all-start.7
  319.0 22.6 %all-to-all-done.7 = bf16[64,3,3072]{2,1,0:T(4,128)(2,1)S(1)} async-done(((bf16[64,3,3072]{2,1,0:T(4,128)(2,1)}), bf16[64,3,3072]{2,1,0:T(4,128)(2,1)S(1)}, u32[]{:S(2)}, u32[]{:S(2)}) %all-to-all-start.7) | async-done | bytes 1179680 | tf_op jit(solution)/shard_map/all_to_all | solution.py:48
  352.4 6.9 all-to-all-start.8
  360.3 22.5 %all-to-all-done.8 = bf16[64,3,3072]{2,1,0:T(4,128)(2,1)} async-done(((bf16[64,3,3072]{2,1,0:T(4,128)(2,1)}), bf16[64,3,3072]{2,1,0:T(4,128)(2,1)}, u32[]{:S(2)}, u32[]{:S(2)}) %all-to-all-start.8) | async-done | bytes 1179680 | tf_op jit(solution)/shard_map/all_to_all | solution.py:41
  386.7 5.5 fusion.2
  400.3 4.9 all-to-all-start.9
  406.4 22.3 %all-to-all-done.9 = bf16[64,3,3072]{2,1,0:T(4,128)(2,1)S(1)} async-done(((bf16[64,3,3072]{2,1,0:T(4,128)(2,1)}), bf16[64,3,3072]{2,1,0:T(4,128)(2,1)S(1)}, u32[]{:S(2)}, u32[]{:S(2)}) %all-to-all-start.9) | async-done | bytes 1179680 | tf_op jit(solution)/shard_map/all_to_all | solution.py:48
  431.6 5.0 collective-permute-done.3
  439.5 7.0 all-to-all-start.10
  446.9 22.9 %all-to-all-done.10 = bf16[64,3,3072]{2,1,0:T(4,128)(2,1)} async-done(((bf16[64,3,3072]{2,1,0:T(4,128)(2,1)}), bf16[64,3,3072]{2,1,0:T(4,128)(2,1)}, u32[]{:S(2)}, u32[]{:S(2)}) %all-to-all-start.10) | async-done | bytes 1179680 | tf_op jit(solution)/shard_map/all_to_all | solution.py:41
  473.8 5.5 fusion
  487.4 5.0 all-to-all-start.11
  494.0 22.0 %all-to-all-done.11 = bf16[64,3,3072]{2,1,0:T(4,128)(2,1)S(1)} async-done(((bf16[64,3,3072]{2,1,0:T(4,128)(2,1)}), bf16[64,3,3072]{2,1,0:T(4,128)(2,1)S(1)}, u32[]{:S(2)}, u32[]{:S(2)}) %all-to-all-start.11) | async-done | bytes 1179680 | tf_op jit(solution)/shard_map/all_to_all | solution.py:48
  517.5 457.7 %all-reduce.2.cloned.1.call-done = f32[1,3072,8]{1,2,0:T(8,128)} async-done(((f32[1,3072,8]{1,2,0:T(8,128)}), f32[1,3072,8]{1,2,0:T(8,128)}) %all-reduce.2.cloned.1.call-update) | async-done | bytes 98320 | tf_op jit(solution)/shard_map/psum | solution.py:222
  (484 shorter events, 148.6 us)
Async XLA Ops:
  13.8 34.0 %all-to-all-start = ((bf16[64,3,3072]{2,1,0:T(4,128)(2,1)}), bf16[64,3,3072]{2,1,0:T(4,128)(2,1)S(1)}, u32[]{:S(2)}, u32[]{:S(2)}) async-start(bf16[64,3,3072]{2,1,0:T(4,128)(2,1)} %bitcast.7), calls=%async_computation | async-start | bytes 3145728 | tf_op jit(solution)/shard_map/all_to_all | solution.py:41
  31.6 36.4 %copy-start.24 = (f32[8,3072]{1,0:T(8,128)}, f32[8,3072]{1,0:T(8,128)S(1)}, u32[]{:S(2)}) copy-start(f32[8,3072]{1,0:T(8,128)S(1)} %bitcast_convert_fusion) | copy-start | bytes 294916
  58.0 40.9 %copy-start.1 = (f32[2,192,1024]{2,1,0:T(8,128)}, f32[2,192,1024]{2,1,0:T(8,128)S(1)}, u32[]{:S(2)}) copy-start(f32[2,192,1024]{2,1,0:T(8,128)S(1)} %get-tuple-element.57) | copy-start | bytes 4718596
  62.3 28.5 %all-to-all-start.1 = ((bf16[64,3,3072]{2,1,0:T(4,128)(2,1)}), bf16[64,3,3072]{2,1,0:T(4,128)(2,1)S(1)}, u32[]{:S(2)}, u32[]{:S(2)}) async-start(bf16[64,3,3072]{2,1,0:T(4,128)(2,1)} %reshape.574), calls=%async_computation.1 | async-start | bytes 3145728 | tf_op jit(solution)/shard_map/all_to_all | solution.py:48
  70.6 22.8 %copy-start.54 = (s32[8,2]{0,1:T(2,128)S(1)}, s32[8,2]{0,1:T(2,128)}, u32[]{:S(2)}) copy-start(s32[8,2]{0,1:T(2,128)} %multiply_add_fusion.5) | copy-start | bytes 196
  93.7 7.7 collective-permute-start
  105.1 29.3 %all-to-all-start.2 = ((bf16[64,3,3072]{2,1,0:T(4,128)(2,1)}), bf16[64,3,3072]{2,1,0:T(4,128)(2,1)}, u32[]{:S(2)}, u32[]{:S(2)}) async-start(bf16[64,3,3072]{2,1,0:T(4,128)(2,1)} %bitcast.17), calls=%async_computation.2 | async-start | bytes 3145728 | tf_op jit(solution)/shard_map/all_to_all | solution.py:41
  149.0 28.5 %all-to-all-start.3 = ((bf16[64,3,3072]{2,1,0:T(4,128)(2,1)}), bf16[64,3,3072]{2,1,0:T(4,128)(2,1)S(1)}, u32[]{:S(2)}, u32[]{:S(2)}) async-start(bf16[64,3,3072]{2,1,0:T(4,128)(2,1)} %reshape.580), calls=%async_computation.3 | async-start | bytes 3145728 | tf_op jit(solution)/shard_map/all_to_all | solution.py:48
  156.5 23.6 %copy-start.53 = (s32[8,2]{0,1:T(2,128)S(1)}, s32[8,2]{0,1:T(2,128)}, u32[]{:S(2)}) copy-start(s32[8,2]{0,1:T(2,128)} %multiply_add_fusion.4) | copy-start | bytes 196
  156.5 29.4 %copy-start.4 = (f32[2,192,1024]{2,1,0:T(8,128)S(1)}, f32[2,192,1024]{2,1,0:T(8,128)}, u32[]{:S(2)}) copy-start(f32[2,192,1024]{2,1,0:T(8,128)} %copy-done.3) | copy-start | bytes 4718596
  181.3 5.8 collective-permute-start.1
  189.6 30.2 %all-to-all-start.4 = ((bf16[64,3,3072]{2,1,0:T(4,128)(2,1)}), bf16[64,3,3072]{2,1,0:T(4,128)(2,1)}, u32[]{:S(2)}, u32[]{:S(2)}) async-start(bf16[64,3,3072]{2,1,0:T(4,128)(2,1)} %bitcast.26), calls=%async_computation.4 | async-start | bytes 3145728 | tf_op jit(solution)/shard_map/all_to_all | solution.py:41
  234.4 28.4 %all-to-all-start.5 = ((bf16[64,3,3072]{2,1,0:T(4,128)(2,1)}), bf16[64,3,3072]{2,1,0:T(4,128)(2,1)S(1)}, u32[]{:S(2)}, u32[]{:S(2)}) async-start(bf16[64,3,3072]{2,1,0:T(4,128)(2,1)} %reshape.586), calls=%async_computation.5 | async-start | bytes 3145728 | tf_op jit(solution)/shard_map/all_to_all | solution.py:48
  241.2 22.8 %copy-start.18 = (f32[2,8,2,3072]{3,1,2,0:T(8,128)S(1)}, f32[2,8,2,3072]{3,1,2,0:T(8,128)}, u32[]{:S(2)}) copy-start(f32[2,8,2,3072]{3,1,2,0:T(8,128)} %copy-done.17) | copy-start | bytes 1179652
  241.2 22.8 %copy-start.35 = (f32[1,8,2,3072]{3,1,2,0:T(8,128)S(1)}, f32[1,8,2,3072]{3,1,2,0:T(8,128)}, u32[]{:S(2)}) copy-start(f32[1,8,2,3072]{3,1,2,0:T(8,128)} %constant_dynamic-slice_fusion.6) | copy-start | bytes 589828
  268.0 37.1 %slice-start = ((s8[6291456]{0:T(1024)(128)(4,1)}), s8[2097152]{0:T(1024)(128)(4,1)S(1)}, s32[]{:S(2)}) async-start(s8[6291456]{0:T(1024)(128)(4,1)} %bitcast.549), calls=%async_computation.13 | async-start | bytes 4194304
  268.0 29.1 %all-to-all-start.6 = ((bf16[64,3,3072]{2,1,0:T(4,128)(2,1)}), bf16[64,3,3072]{2,1,0:T(4,128)(2,1)}, u32[]{:S(2)}, u32[]{:S(2)}) async-start(bf16[64,3,3072]{2,1,0:T(4,128)(2,1)} %bitcast.569), calls=%async_computation.6 | async-start | bytes 3145728 | tf_op jit(solution)/shard_map/all_to_all | solution.py:41
  313.3 28.4 %all-to-all-start.7 = ((bf16[64,3,3072]{2,1,0:T(4,128)(2,1)}), bf16[64,3,3072]{2,1,0:T(4,128)(2,1)S(1)}, u32[]{:S(2)}, u32[]{:S(2)}) async-start(bf16[64,3,3072]{2,1,0:T(4,128)(2,1)} %reshape.592), calls=%async_computation.7 | async-start | bytes 3145728 | tf_op jit(solution)/shard_map/all_to_all | solution.py:48
  319.0 24.1 %copy-start.39 = (bf16[2,8,3072]{2,1,0:T(8,128)(2,1)S(1)}, bf16[2,8,3072]{2,1,0:T(8,128)(2,1)}, u32[]{:S(2)}) copy-start(bf16[2,8,3072]{2,1,0:T(8,128)(2,1)} %param.11) | copy-start | bytes 294916
  319.0 24.1 %copy-start.59 = (f32[8]{0:T(128)S(1)}, f32[8]{0:T(128)}, u32[]{:S(2)}) copy-start(f32[8]{0:T(128)} %copy-done.58) | copy-start | bytes 100
  319.0 24.1 %copy-start.70 = (f32[8]{0:T(128)S(1)}, f32[8]{0:T(128)}, u32[]{:S(2)}) copy-start(f32[8]{0:T(128)} %get-tuple-element.49) | copy-start | bytes 100
  343.2 6.3 collective-permute-start.2
  352.4 39.8 %slice-start.2 = ((s8[6291456]{0:T(1024)(128)(4,1)}), s8[2097152]{0:T(1024)(128)(4,1)S(1)}, s32[]{:S(2)}) async-start(s8[6291456]{0:T(1024)(128)(4,1)} %bitcast.551), calls=%async_computation.15 | async-start | bytes 4194304
  352.4 30.3 %all-to-all-start.8 = ((bf16[64,3,3072]{2,1,0:T(4,128)(2,1)}), bf16[64,3,3072]{2,1,0:T(4,128)(2,1)}, u32[]{:S(2)}, u32[]{:S(2)}) async-start(bf16[64,3,3072]{2,1,0:T(4,128)(2,1)} %bitcast.567), calls=%async_computation.8 | async-start | bytes 3145728 | tf_op jit(solution)/shard_map/all_to_all | solution.py:41
  400.3 28.4 %all-to-all-start.9 = ((bf16[64,3,3072]{2,1,0:T(4,128)(2,1)}), bf16[64,3,3072]{2,1,0:T(4,128)(2,1)S(1)}, u32[]{:S(2)}, u32[]{:S(2)}) async-start(bf16[64,3,3072]{2,1,0:T(4,128)(2,1)} %reshape.598), calls=%async_computation.9 | async-start | bytes 3145728 | tf_op jit(solution)/shard_map/all_to_all | solution.py:48
  430.3 6.3 collective-permute-start.3
  439.4 39.8 %slice-start.4 = ((s8[6291456]{0:T(1024)(128)(4,1)}), s8[2097152]{0:T(1024)(128)(4,1)S(1)}, s32[]{:S(2)}) async-start(s8[6291456]{0:T(1024)(128)(4,1)} %bitcast.553), calls=%async_computation.17 | async-start | bytes 4194304
  439.5 30.4 %all-to-all-start.10 = ((bf16[64,3,3072]{2,1,0:T(4,128)(2,1)}), bf16[64,3,3072]{2,1,0:T(4,128)(2,1)}, u32[]{:S(2)}, u32[]{:S(2)}) async-start(bf16[64,3,3072]{2,1,0:T(4,128)(2,1)} %bitcast.568), calls=%async_computation.10 | async-start | bytes 3145728 | tf_op jit(solution)/shard_map/all_to_all | solution.py:41
  487.4 28.5 %all-to-all-start.11 = ((bf16[64,3,3072]{2,1,0:T(4,128)(2,1)}), bf16[64,3,3072]{2,1,0:T(4,128)(2,1)S(1)}, u32[]{:S(2)}, u32[]{:S(2)}) async-start(bf16[64,3,3072]{2,1,0:T(4,128)(2,1)} %reshape.604), calls=%async_computation.11 | async-start | bytes 3145728 | tf_op jit(solution)/shard_map/all_to_all | solution.py:48
  492.4 482.8 %all-reduce.2.cloned.1.call-start = ((), (), s32[]{:S(2)}) async-start(), calls=%async_computation.12 | async-start | bytes 196608 | tf_op jit(solution)/shard_map/psum | solution.py:222
  492.5 24.3 %copy-start.43 = (bf16[1,2,8,3072]{3,2,1,0:T(8,128)(2,1)}, bf16[1,2,8,3072]{3,2,1,0:T(8,128)(2,1)S(1)}, u32[]{:S(2)}) copy-start(bf16[1,2,8,3072]{3,2,1,0:T(8,128)(2,1)S(1)} %fusion.176) | copy-start | bytes 294916
  517.5 459.3 %copy-start.42 = (bf16[1,2,8,3072]{3,2,1,0:T(8,128)(2,1)}, bf16[1,2,8,3072]{3,2,1,0:T(8,128)(2,1)S(1)}, u32[]{:S(2)}) copy-start(bf16[1,2,8,3072]{3,2,1,0:T(8,128)(2,1)S(1)} %fusion.188) | copy-start | bytes 294916
  (80 other events, 454.3 us)
Sparse Core Ops, SparseCore 0:
  496.3 478.9 all-reduce.1
where the time goes:
time: 996 us; the launch traced here: 984 us
  waiting for transfers between devices  719 us (72%)
  starting transfers between devices  85.1 us (9%)
  local copies, waits for them, and re-layouts  79.4 us (8%)
  matrix products  65.2 us (7%)
  other arithmetic  19.5 us (2%)
  between operations  16.4 us (2%)
    psum x1, waiting for transfers between devices, per_device(): router_total = lax.psum(router_sum, ('expert', 'dp'))  458 us
    all_to_all x6, waiting for transfers between devices, collect(): lax.all_to_all(partial_out.reshape(experts * replicas, capacity, model_wi...  128 us
    all_to_all x6, waiting for transfers between devices, deliver(): lax.all_to_all(tiled, ('expert', 'dp'), split_axis=0, concat_axis=0, tile...  124 us
    all_to_all x6, starting transfers between devices, deliver(): lax.all_to_all(tiled, ('expert', 'dp'), split_axis=0, concat_axis=0, tile...  42.9 us
    all_to_all x6, starting transfers between devices, collect(): lax.all_to_all(partial_out.reshape(experts * replicas, capacity, model_wi...  29.7 us
  transfers between devices with their start and end apart: 17, of which 16 were waited for; matrix products, arithmetic and copies ran while one was open for 3% of the time, Pallas kernels for 0%

commit v1 on v0

v1 whole, which is shorter than its diff:
```python
import jax
import jax.numpy as jnp
from jax import lax
from jax.experimental import pallas as pl
from jax.experimental.pallas import tpu as pltpu
from jax.sharding import PartitionSpec as P

EPSILON = 1e-05
MESH = pl.DeviceIdType.MESH
NT = (((1,), (1,)), ((), ()))


def sigmoid(x):
    return jax.nn.sigmoid(x)


def relay_kernel(
    dims,
    table,
    x_in,
    cot_in,
    gain_in,
    router_in,
    wg_hbm,
    wu_hbm,
    wd_hbm,
    acts,
    grads,
    rgrad,
    wg,
    wu,
    wd,
    lin,
    ups,
    hid,
    scl,
    prob,
    pdiff,
    snd,
    disp,
    xf,
    xb,
    gs,
    us,
    act,
    act2,
    obuf,
    osend,
    orecv,
    snd2,
    comb,
    racc,
    r1,
    r2,
    r3,
    rsrc,
    w_sem,
    disp_send,
    disp_recv,
    x_send,
    x_recv,
    o_send,
    o_recv,
    comb_send,
    comb_recv,
    hop_send,
    hop_recv,
    r_send,
    r_recv,
):
    n_exp, n_x, cap, toks, chunks, n_ff, n_out, width = dims
    group = n_exp * n_x
    rows = group * cap
    per_x = cap * chunks
    inv_count = 1.0 / (chunks * 128)
    n_group, k_group = xb.shape[1], xb.shape[4]
    group_chunks = k_group // 128
    none = 2 * toks

    section = lax.axis_index("section")
    my_e = lax.axis_index("expert")
    my_dp = lax.axis_index("dp")
    my_x = my_dp // 2
    core = lax.rem(my_dp, 2)
    me = my_e * n_x + my_x

    def peer(step):
        q = lax.rem(me + step, group)
        return q, {"expert": q // n_x, "dp": lax.rem(q, n_x) * 2 + core}

    sibling = {"dp": my_x * 2 + 1 - core}
    partner = {"section": 1 - section}

    weights = [
        pltpu.make_async_copy(src, dst, w_sem.at[i])
        for i, (src, dst) in enumerate(((wg_hbm, wg), (wu_hbm, wu), (wd_hbm, wd)))
    ]
    for copy in weights:
        copy.start()

    barrier = pltpu.get_barrier_semaphore()

    @pl.loop(1, group)
    def _(step):
        _, where = peer(step)
        pl.semaphore_signal(barrier, inc=1, device_id=where, device_id_type=MESH)

    @pl.loop(0, n_x)
    def _(x):
        pl.semaphore_signal(
            barrier, inc=1, device_id={"dp": x * 2 + 1 - core}, device_id_type=MESH
        )

    pl.semaphore_signal(barrier, inc=1, device_id=partner, device_id_type=MESH)

    @pl.when(section == 0)
    def _():
        lin[...] = x_in[...]

    @pl.when(section == 1)
    def _():
        ups[...] = cot_in[...]

    hid[:, toks] = jnp.zeros_like(hid[:, toks])
    scl[:, none] = jnp.zeros_like(scl[:, none])
    pl.semaphore_wait(barrier, group + n_x)

    gain = gain_in[...]

    def total(v):
        return jnp.sum(v, axis=(0, 1), keepdims=True)

    def inv_rms_of(v):
        return lax.rsqrt(total(v * v) * inv_count + EPSILON)

    def wait_bytes(ref, sem):
        pltpu.make_async_copy(ref, ref, sem).wait()

    def route(m, t, k):
        return table[m, n_exp * cap + none + 2 * t + k]

    def router_diff(m, t):
        return router_in[route(m, t, 0)] - router_in[route(m, t, 1)]

    def send_dispatch(phase):
        own = pltpu.make_async_copy(snd.at[phase, my_e], disp.at[phase, me], disp_recv.at[phase])
        own.start()

        @pl.loop(1, group)
        def _(step):
            q, where = peer(step)
            pltpu.make_async_remote_copy(
                src_ref=snd.at[phase, q // n_x],
                dst_ref=disp.at[phase, me],
                send_sem=disp_send.at[phase],
                recv_sem=disp_recv.at[phase],
                device_id=where,
                device_id_type=MESH,
            ).start()

    def send_combine(phase):
        own = pltpu.make_async_copy(snd2.at[phase, me], comb.at[phase, me], comb_recv.at[phase])
        own.start()

        @pl.loop(1, group)
        def _(step):
            q, where = peer(step)
            pltpu.make_async_remote_copy(
                src_ref=snd2.at[phase, q],
                dst_ref=comb.at[phase, me],
                send_sem=comb_send.at[phase],
                recv_sem=comb_recv.at[phase],
                device_id=where,
                device_id_type=MESH,
            ).start()

    def hop(ref, dst, which, m):
        return pltpu.make_async_remote_copy(
            src_ref=ref.at[m],
            dst_ref=dst.at[m],
            send_sem=hop_send.at[which, m],
            recv_sem=hop_recv.at[which, m],
            device_id=partner,
            device_id_type=MESH,
        )

    def take_rows(phase):
        wait_bytes(disp.at[phase], disp_recv.at[phase])

        @pl.loop(0, group)
        def _(q):
            block = disp[phase, q].astype(jnp.float32).reshape(per_x, 128)
            xf[pl.ds(pl.multiple_of(q * per_x, 8), per_x), :] = block

        for g in range(n_group):
            for i in range(group_chunks):
                part = xf[pl.ds(g * group_chunks + i, rows, stride=chunks), :]
                xb[phase, g, core, :, i * 128 : (i + 1) * 128] = part.astype(jnp.bfloat16)
            pltpu.make_async_remote_copy(
                src_ref=xb.at[phase, g, core],
                dst_ref=xb.at[phase, g, core],
                send_sem=x_send.at[phase, g],
                recv_sem=x_recv.at[phase, g],
                device_id=sibling,
                device_id_type=MESH,
            ).start()
        for g in range(n_group):
            wait_bytes(xb.at[phase, g, 1 - core], x_recv.at[phase, g])

    def left(phase, g):
        return xb[phase, g].reshape(2 * rows, k_group)

    def share_tile(phase, n, tile):
        obuf[n] = tile.reshape(2, rows, 256)
        osend[phase, n] = obuf[n, 1 - core].astype(jnp.bfloat16)
        pltpu.make_async_remote_copy(
            src_ref=osend.at[phase, n],
            dst_ref=orecv.at[phase, n],
            send_sem=o_send.at[phase],
            recv_sem=o_recv.at[phase],
            device_id=sibling,
            device_id_type=MESH,
        ).start()

    def give_back(phase):
        wait_bytes(orecv.at[phase], o_recv.at[phase])
        for n in range(n_out):
            both = obuf[n, core] + orecv[phase, n].astype(jnp.float32)
            for i in range(2):
                xf[pl.ds(2 * n + i, rows, stride=chunks), :] = both[:, i * 128 : (i + 1) * 128]

        @pl.loop(0, group)
        def _(q):
            block = xf[pl.ds(pl.multiple_of(q * per_x, 8), per_x), :]
            snd2[phase, q] = block.reshape(cap, chunks, 128).astype(jnp.bfloat16)

        send_combine(phase)

    def fill_slots(phase, m, source, shift):
        for e in range(n_exp):
            for s in range(cap):
                snd[phase, e, s] = source[m, table[m, e * cap + s] >> shift]

    def picked_of(phase, m, t, k):
        slot = table[m, n_exp * cap + 2 * t + k]
        e, s = slot // cap, lax.rem(slot, cap)
        result = comb[phase, e * n_x, s].astype(jnp.float32)
        for x in range(1, n_x):
            result = result + comb[phase, e * n_x + x, s].astype(jnp.float32)
        return result

    def forward_send(m):
        @pl.when(section == 1)
        def _():
            hop(acts, lin, 0, m).wait_recv()

        for t in range(toks):
            v = lin[m, t].astype(jnp.float32)
            hidden = (v * inv_rms_of(v) * gain).astype(jnp.bfloat16)
            hid[m, t] = hidden
            gap = total(hidden.astype(jnp.float32) * router_diff(m, t))
            prob[m, t, 0] = jnp.broadcast_to(sigmoid(gap), (8, 128))
            prob[m, t, 1] = jnp.broadcast_to(sigmoid(-gap), (8, 128))
        fill_slots(m, m, hid, 1)
        send_dispatch(m)

    def forward_expert(m):
        take_rows(m)
        if m == 0:
            weights[0].wait()
            weights[1].wait()

        @pl.loop(0, n_ff)
        def _(n):
            cols = pl.ds(pl.multiple_of(n * 256, 256), 256)
            gate = jnp.zeros((2 * rows, 256), jnp.float32)
            up = jnp.zeros((2 * rows, 256), jnp.float32)
            for g in range(n_group):
                x = left(m, g)
                k = slice(g * k_group, (g + 1) * k_group)
                gate = gate + jnp.dot(x, wg[k, cols], preferred_element_type=jnp.float32)
                up = up + jnp.dot(x, wu[k, cols], preferred_element_type=jnp.float32)
            gs[m, n] = gate
            us[m, n] = up
            act[n] = (gate * sigmoid(gate) * up).astype(jnp.bfloat16)

        if m == 0:
            weights[2].wait()

        @pl.loop(0, n_out)
        def _(n):
            cols = pl.ds(pl.multiple_of(n * 256, 256), 256)
            tile = jnp.zeros((2 * rows, 256), jnp.float32)
            for k in range(n_ff):
                tile = tile + jnp.dot(
                    act[k], wd[k * 256 : (k + 1) * 256, cols], preferred_element_type=jnp.float32
                )
            share_tile(m, n, tile)

        give_back(m)

    def forward_end(m):
        wait_bytes(comb.at[m], comb_recv.at[m])
        for t in range(toks):
            p0 = prob[m, t, 0, 0:1, 0:1]
            p1 = prob[m, t, 1, 0:1, 0:1]
            one, two = picked_of(m, m, t, 0), picked_of(m, m, t, 1)
            v = lin[m, t].astype(jnp.float32)
            acts[m, t] = (v + (p0 * one + p1 * two)).astype(jnp.bfloat16)
            pdiff[m, t] = one - two

        @pl.when(section == 0)
        def _():
            hop(acts, lin, 0, m).start()

    def backward_send(m):
        phase = 2 + m

        @pl.when(section == 0)
        def _():
            hop(grads, ups, 1, m).wait_recv()

        gaps = []
        for t in range(toks):
            up = ups[m, t].astype(jnp.float32)
            p0 = prob[m, t, 0, 0:1, 0:1]
            p1 = prob[m, t, 1, 0:1, 0:1]
            d_gap = p0 * p1 * total(up * pdiff[m, t])
            prob[m, t, 2] = jnp.broadcast_to(d_gap, (8, 128))
            gaps.append(d_gap)
            scl[m, 2 * t] = (p0 * up).astype(jnp.bfloat16)
            scl[m, 2 * t + 1] = (p1 * up).astype(jnp.bfloat16)
        fill_slots(phase, m, scl, 0)
        send_dispatch(phase)
        for e in range(n_exp):
            term = racc[e] if m else jnp.zeros((chunks, 128), jnp.float32)
            for t in range(toks):
                sign = jnp.where(route(m, t, 0) == e, 1.0, 0.0) - jnp.where(
                    route(m, t, 1) == e, 1.0, 0.0
                )
                term = term + (gaps[t] * sign) * hid[m, t].astype(jnp.float32)
            racc[e] = term

    def router_one():
        pltpu.make_async_copy(racc.at[my_e], r1.at[my_e], r_recv.at[0]).start()

        @pl.loop(1, n_exp)
        def _(step):
            e = lax.rem(my_e + step, n_exp)
            pltpu.make_async_remote_copy(
                src_ref=racc.at[e],
                dst_ref=r1.at[my_e],
                send_sem=r_send.at[0],
                recv_sem=r_recv.at[0],
                device_id={"expert": e},
                device_id_type=MESH,
            ).start()

    def router_two():
        wait_bytes(r1, r_recv.at[0])
        rsrc[0] = jnp.sum(r1[...], axis=0)
        pltpu.make_async_copy(rsrc.at[0], r2.at[my_dp], r_recv.at[1]).start()

        @pl.loop(1, 2 * n_x)
        def _(step):
            dp = lax.rem(my_dp + step, 2 * n_x)
            pltpu.make_async_remote_copy(
                src_ref=rsrc.at[0],
                dst_ref=r2.at[my_dp],
                send_sem=r_send.at[1],
                recv_sem=r_recv.at[1],
                device_id={"dp": dp},
                device_id_type=MESH,
            ).start()

    def router_three():
        wait_bytes(r2, r_recv.at[1])
        rsrc[1] = jnp.sum(r2[...], axis=0)
        pltpu.make_async_copy(rsrc.at[1], r3.at[my_e], r_recv.at[2]).start()

        @pl.loop(1, n_exp)
        def _(step):
            e = lax.rem(my_e + step, n_exp)
            pltpu.make_async_remote_copy(
                src_ref=rsrc.at[1],
                dst_ref=r3.at[my_e],
                send_sem=r_send.at[2],
                recv_sem=r_recv.at[2],
                device_id={"expert": e},
                device_id_type=MESH,
            ).start()

    def backward_expert(m):
        phase = 2 + m
        take_rows(phase)

        @pl.loop(0, n_ff)
        def _(n):
            part = pl.ds(pl.multiple_of(n * 256, 256), 256)
            d_act = jnp.zeros((2 * rows, 256), jnp.float32)
            for g in range(n_group):
                d_act = d_act + lax.dot_general(
                    left(phase, g),
                    wd[part, g * k_group : (g + 1) * k_group],
                    NT,
                    preferred_element_type=jnp.float32,
                )
            gate, up = gs[m, n], us[m, n]
            sig = sigmoid(gate)
            act[n] = (d_act * up * sig * (1.0 + gate * (1.0 - sig))).astype(jnp.bfloat16)
            act2[n] = (d_act * gate * sig).astype(jnp.bfloat16)

        if m:
            router_two()

        @pl.loop(0, n_out)
        def _(n):
            part = pl.ds(pl.multiple_of(n * 256, 256), 256)
            tile = jnp.zeros((2 * rows, 256), jnp.float32)
            for k in range(n_ff):
                cols = slice(k * 256, (k + 1) * 256)
                tile = tile + lax.dot_general(
                    act[k], wg[part, cols], NT, preferred_element_type=jnp.float32
                )
                tile = tile + lax.dot_general(
                    act2[k], wu[part, cols], NT, preferred_element_type=jnp.float32
                )
            share_tile(phase, n, tile)

        give_back(phase)
        if m:
            router_three()

    def backward_end(m):
        phase = 2 + m
        wait_bytes(comb.at[phase], comb_recv.at[phase])
        for t in range(toks):
            d_gap = prob[m, t, 2, 0:1, 0:1]
            d_hidden = picked_of(phase, m, t, 0) + picked_of(phase, m, t, 1)
            d_hidden = d_hidden + d_gap * router_diff(m, t)
            v = lin[m, t].astype(jnp.float32)
            up = ups[m, t].astype(jnp.float32)
            inv_rms = inv_rms_of(v)
            weighted = gain * d_hidden
            mean = total(v * weighted) * inv_count
            d_in = up + inv_rms * weighted - v * (inv_rms * inv_rms * inv_rms) * mean
            grads[m, t] = d_in.astype(jnp.bfloat16)

        @pl.when(section == 1)
        def _():
            hop(grads, ups, 1, m).start()

    for m in range(2):
        forward_send(m)
        forward_expert(m)
        forward_end(m)
    for m in range(2):
        backward_send(m)
        if m:
            router_one()
        backward_expert(m)
        backward_end(m)
    wait_bytes(r3, r_recv.at[2])
    rgrad[...] = r3[...]

    for phase in range(4):
        wait_bytes(disp.at[phase, pl.ds(0, group - 1)], disp_send.at[phase])
        wait_bytes(comb.at[phase, pl.ds(0, group - 1)], comb_send.at[phase])
        for g in range(n_group):
            wait_bytes(xb.at[phase, g, core], x_send.at[phase, g])
        wait_bytes(osend.at[phase], o_send.at[phase])
    wait_bytes(r1.at[pl.ds(0, n_exp - 1)], r_send.at[0])
    wait_bytes(r2.at[pl.ds(0, 2 * n_x - 1)], r_send.at[1])
    wait_bytes(r1.at[pl.ds(0, n_exp - 1)], r_send.at[2])
    for m in range(2):

        @pl.when(section == 0)
        def _():
            hop(acts, lin, 0, m).wait_send()

        @pl.when(section == 1)
        def _():
            hop(grads, ups, 1, m).wait_send()


def slot_tables(picks, cap, experts):
    micro, toks, top = picks.shape
    flat = picks.reshape(micro, toks * top)
    order = jnp.arange(toks * top, dtype=jnp.int32)
    same = (flat[:, :, None] == flat[:, None, :]) & (order[None, None, :] < order[None, :, None])
    slot_of = flat * cap + jnp.sum(same.astype(jnp.int32), axis=2)
    slots = jnp.arange(experts * cap, dtype=jnp.int32)
    hit = slot_of[:, None, :] == slots[None, :, None]
    gap = toks * top - order
    slot_src = toks * top - jnp.sum(jnp.where(hit, gap[None, None, :], 0), axis=2)
    return jnp.concatenate([slot_src, slot_of, flat], axis=1).astype(jnp.int32)


def per_device(inputs, cotangent, norm_gain, router, w_gate, w_up, w_down, routes):
    micro, toks, width = inputs.shape
    experts = router.shape[2]
    dp = lax.axis_size("dp")
    n_exp, n_x = lax.axis_size("expert"), dp // 2
    cap = 3
    chunks = width // 128
    hidden_units = w_gate.shape[3]
    n_ff, n_out = hidden_units // 256, width // 256
    group = n_exp * n_x
    rows = group * cap
    n_group = 4
    k_group = width // n_group
    table = slot_tables(routes[0], cap, experts)
    bf, f32 = jnp.bfloat16, jnp.float32
    block = (chunks, 128)
    dma = pltpu.SemaphoreType.DMA
    scratch = [
        pltpu.VMEM((width, hidden_units), bf),
        pltpu.VMEM((width, hidden_units), bf),
        pltpu.VMEM((hidden_units, width), bf),
        pltpu.VMEM((micro, toks) + block, bf),
        pltpu.VMEM((micro, toks) + block, bf),
        pltpu.VMEM((micro, toks + 1) + block, bf),
        pltpu.VMEM((micro, 2 * toks + 1) + block, bf),
        pltpu.VMEM((micro, toks, 3, 8, 128), f32),
        pltpu.VMEM((micro, toks) + block, f32),
        pltpu.VMEM((4, n_exp, cap) + block, bf),
        pltpu.VMEM((4, group, cap) + block, bf),
        pltpu.VMEM((rows * chunks, 128), f32),
        pltpu.VMEM((4, n_group, 2, rows, k_group), bf),
        pltpu.VMEM((micro, n_ff, 2 * rows, 256), f32),
        pltpu.VMEM((micro, n_ff, 2 * rows, 256), f32),
        pltpu.VMEM((n_ff, 2 * rows, 256), bf),
        pltpu.VMEM((n_ff, 2 * rows, 256), bf),
        pltpu.VMEM((n_out, 2, rows, 256), f32),
        pltpu.VMEM((4, n_out, rows, 256), bf),
        pltpu.VMEM((4, n_out, rows, 256), bf),
        pltpu.VMEM((4, group, cap) + block, bf),
        pltpu.VMEM((4, group, cap) + block, bf),
        pltpu.VMEM((n_exp,) + block, f32),
        pltpu.VMEM((n_exp,) + block, f32),
        pltpu.VMEM((dp,) + block, f32),
        pltpu.VMEM((n_exp,) + block, f32),
        pltpu.VMEM((2,) + block, f32),
        dma((3,)),
        dma((4,)),
        dma((4,)),
        dma((4, n_group)),
        dma((4, n_group)),
        dma((4,)),
        dma((4,)),
        dma((4,)),
        dma((4,)),
        dma((2, micro)),
        dma((2, micro)),
        dma((3,)),
        dma((3,)),
    ]
    dims = (n_exp, n_x, cap, toks, chunks, n_ff, n_out, width)
    vmem = pl.BlockSpec(memory_space=pltpu.VMEM)
    hbm = pl.BlockSpec(memory_space=pl.ANY)
    acts, grads, rgrad = pl.pallas_call(
        lambda *refs: relay_kernel(dims, *refs),
        out_shape=(
            jax.ShapeDtypeStruct((micro, toks) + block, bf),
            jax.ShapeDtypeStruct((micro, toks) + block, bf),
            jax.ShapeDtypeStruct((experts,) + block, f32),
        ),
        in_specs=[pl.BlockSpec(memory_space=pltpu.SMEM)] + [vmem] * 4 + [hbm] * 3,
        out_specs=(vmem, vmem, vmem),
        scratch_shapes=scratch,
        compiler_params=pltpu.CompilerParams(
            collective_id=0, has_side_effects=True, vmem_limit_bytes=63 * 1024 * 1024
        ),
        name="relay",
    )(
        table,
        inputs.reshape((micro, toks) + block),
        cotangent.reshape((micro, toks) + block),
        norm_gain[0].astype(f32).reshape(block),
        router[0].astype(f32).T.reshape((experts,) + block),
        w_gate[0, 0],
        w_up[0, 0],
        w_down[0, 0],
    )
    return (
        acts.reshape(1, micro, toks, width),
        grads.reshape(1, micro, toks, width),
        rgrad.reshape(experts, width).T[None],
    )


def solution(mesh):
    placed = (
        P(None, ("expert", "dp"), None),
        P(None, ("expert", "dp"), None),
        P("section", None),
        P("section", None, None),
        P("section", "expert", None, "dp"),
        P("section", "expert", None, "dp"),
        P("section", "expert", "dp", None),
        P("section", None, ("expert", "dp"), None),
    )
    return jax.shard_map(
        per_device,
        mesh=mesh,
        in_specs=placed,
        out_specs=(
            P("section", None, ("expert", "dp"), None),
            P("section", None, ("expert", "dp"), None),
            P("section", None, None),
        ),
        check_vma=False,
    )
```

time: 996 us -> 220 us (0.22); the launches traced: 984 us -> 219 us
  waiting for transfers between devices: 719 us -> 0 us
  Pallas kernels: 0 us -> 207 us
  starting transfers between devices: 85.1 us -> 0 us
  local copies, waits for them, and re-layouts: 79.4 us -> 7.85 us
  matrix products: 65.2 us -> 0 us
  other arithmetic: 19.5 us -> 3.1 us
  between operations: 16.4 us -> 0.66 us
    psum x1 -> x0, waiting for transfers between devices: 458 us -> none  [per_device(): router_total = lax.psum(router_sum, ('expert', 'dp'))]
    all_to_all x12 -> x0, waiting for transfers between devices: 252 us -> none  [the longest x6 128 us: collect(): lax.all_to_all(partial_out.reshape(experts * replicas, capacity, model_wi...]
    pallas_call x0 -> x1, Pallas kernels: none -> 207 us  [per_device(): pl.pallas_call(lambda *refs: relay_kernel(dims, *refs), out_shape=(jax.Sh...]
    all_to_all x12 -> x0, starting transfers between devices: 72.6 us -> none  [the longest x6 42.9 us: deliver(): lax.all_to_all(tiled, ('expert', 'dp'), split_axis=0, concat_axis=0, tile...]
    dot_general x42 -> x0, matrix products: 65.2 us -> none  [the longest x3 16.2 us: backward_layer(): lax.dot_general(arrived, down_w, contract_last, preferred_element_type=jn...]
    reshape x30 -> x3, local copies, waits for them, and re-layouts: 33.9 us -> 4.8 us  [the longest x1 1.64 us: per_device(): cotangent.reshape((micro, toks) + block)]
    ppermute x4 -> x0, starting transfers between devices: 12.4 us -> none  [passed_along(): return lax.ppermute(block, axis, route)]
    dynamic_slice x17 -> x0, local copies, waits for them, and re-layouts: 10.4 us -> none  [the longest x9 7.71 us: store_micro(): previous = lax.dynamic_index_in_dim(stored, which_mb, 0, keepdims=False)]
  transfers between devices with their start and end apart: 17 -> 0, of which waited for: 16 -> 0; matrix products, arithmetic and copies ran while one was open for 3% -> 0% of each run, Pallas kernels for 0% -> 0%
where the time goes in v1:
time: 220 us; the launch traced here: 219 us
  Pallas kernels  207 us (94%)
  local copies, waits for them, and re-layouts  7.85 us (4%)
  other arithmetic  3.1 us (1%)
    pallas_call x1, Pallas kernels, per_device(): pl.pallas_call(lambda *refs: relay_kernel(dims, *refs), out_shape=(jax.Sh...  207 us

profile of v1, /device:TPU:1, one launch (start us, length us, event | category | flops | bytes accessed | tf_op | source)
XLA Modules:
  0.0 218.9 jit_solution(1247802098956213273)
XLA Ops:
  0.7 0.8 copy.13
  1.4 0.1 reshape_squeeze.3
  1.5 0.2 convert_reduce_fusion
  1.7 0.1 select_reduce_fusion
  1.8 0.7 pad_add_fusion.refs_0_
  2.5 1.3 convert_element_type.18
  3.8 0.8 convert_bitcast_fusion
  4.6 0.7 copy.23
  5.3 1.6 copy_bitcast_fusion.1
  6.9 207.3 %relay.1 = (bf16[2,8,24,128]{3,2,1,0:T(8,128)(2,1)}, bf16[2,8,24,128]{3,2,1,0:T(8,128)(2,1)}, f32[8,24,128]{2,1,0:T(8,128)}) custom-call(s32[2,56]{1,0:T(2,128)} %pad_add_fusion.refs_0_, bf16[2,8,24,128]{3,2,1,0:T(8,128)(2,1)} %get-tuple-element.10.refs_1_, bf16[2,8,24,128]{3,2,1,0:T(8,128)(2,1)} %get-tuple-element.9.refs_2_, f32[24,128]{1,0:T(8,128)} %bitcast.46, ...), custom_call_target="tpu_custom_call" | custom-call | tf_op jit(solution)/shard_map/relay/pallas_call | solution.py:561
  214.2 1.6 reshape.65
  215.8 1.6 reshape.66
  217.4 1.6 copy.22
  (4 shorter events, 0.0 us)

commit v2 on v1

--- a/solution.py
+++ b/solution.py
@@ -48,7 +48,10 @@
     osend,
     orecv,
     snd2,
-    comb,
+    comb_0,
+    comb_1,
+    comb_2,
+    comb_3,
     racc,
     r1,
     r2,
@@ -84,6 +87,8 @@
     core = lax.rem(my_dp, 2)
     me = my_e * n_x + my_x
 
+    comb = (comb_0, comb_1, comb_2, comb_3)
+
     def peer(step):
         q = lax.rem(me + step, group)
         return q, {"expert": q // n_x, "dp": lax.rem(q, n_x) * 2 + core}
@@ -159,7 +164,7 @@
             ).start()
 
     def send_combine(phase):
-        own = pltpu.make_async_copy(snd2.at[phase, me], comb.at[phase, me], comb_recv.at[phase])
+        own = pltpu.make_async_copy(snd2.at[phase, me], comb[phase].at[me], comb_recv.at[phase])
         own.start()
 
         @pl.loop(1, group)
@@ -167,7 +172,7 @@
             q, where = peer(step)
             pltpu.make_async_remote_copy(
                 src_ref=snd2.at[phase, q],
-                dst_ref=comb.at[phase, me],
+                dst_ref=comb[phase].at[me],
                 send_sem=comb_send.at[phase],
                 recv_sem=comb_recv.at[phase],
                 device_id=where,
@@ -204,6 +209,8 @@
                 device_id=sibling,
                 device_id_type=MESH,
             ).start()
+
+    def sibling_rows(phase):
         for g in range(n_group):
             wait_bytes(xb.at[phase, g, 1 - core], x_recv.at[phase, g])
 
@@ -244,12 +251,12 @@
     def picked_of(phase, m, t, k):
         slot = table[m, n_exp * cap + 2 * t + k]
         e, s = slot // cap, lax.rem(slot, cap)
-        result = comb[phase, e * n_x, s].astype(jnp.float32)
+        result = comb[phase][e * n_x, s].astype(jnp.float32)
         for x in range(1, n_x):
-            result = result + comb[phase, e * n_x + x, s].astype(jnp.float32)
+            result = result + comb[phase][e * n_x + x, s].astype(jnp.float32)
         return result
 
-    def forward_send(m):
+    def forward_ready(m):
         @pl.when(section == 1)
         def _():
             hop(acts, lin, 0, m).wait_recv()
@@ -262,10 +269,9 @@
             prob[m, t, 0] = jnp.broadcast_to(sigmoid(gap), (8, 128))
             prob[m, t, 1] = jnp.broadcast_to(sigmoid(-gap), (8, 128))
         fill_slots(m, m, hid, 1)
-        send_dispatch(m)
 
     def forward_expert(m):
-        take_rows(m)
+        sibling_rows(m)
         if m == 0:
             weights[0].wait()
             weights[1].wait()
@@ -297,10 +303,8 @@
                 )
             share_tile(m, n, tile)
 
-        give_back(m)
-
     def forward_end(m):
-        wait_bytes(comb.at[m], comb_recv.at[m])
+        wait_bytes(comb[m], comb_recv.at[m])
         for t in range(toks):
             p0 = prob[m, t, 0, 0:1, 0:1]
             p1 = prob[m, t, 1, 0:1, 0:1]
@@ -340,6 +344,8 @@
                 )
                 term = term + (gaps[t] * sign) * hid[m, t].astype(jnp.float32)
             racc[e] = term
+        if m:
+            router_one()
 
     def router_one():
         pltpu.make_async_copy(racc.at[my_e], r1.at[my_e], r_recv.at[0]).start()
@@ -392,7 +398,7 @@
 
     def backward_expert(m):
         phase = 2 + m
-        take_rows(phase)
+        sibling_rows(phase)
 
         @pl.loop(0, n_ff)
         def _(n):
@@ -427,13 +433,9 @@
                 )
             share_tile(phase, n, tile)
 
-        give_back(phase)
-        if m:
-            router_three()
-
     def backward_end(m):
         phase = 2 + m
-        wait_bytes(comb.at[phase], comb_recv.at[phase])
+        wait_bytes(comb[phase], comb_recv.at[phase])
         for t in range(toks):
             d_gap = prob[m, t, 2, 0:1, 0:1]
             d_hidden = picked_of(phase, m, t, 0) + picked_of(phase, m, t, 1)
@@ -450,22 +452,64 @@
         def _():
             hop(grads, ups, 1, m).start()
 
-    for m in range(2):
-        forward_send(m)
-        forward_expert(m)
-        forward_end(m)
-    for m in range(2):
-        backward_send(m)
-        if m:
-            router_one()
-        backward_expert(m)
-        backward_end(m)
+    @pl.when(section == 0)
+    def _():
+        forward_ready(0)
+        send_dispatch(0)
+        forward_ready(1)
+        take_rows(0)
+        send_dispatch(1)
+        forward_expert(0)
+        give_back(0)
+        take_rows(1)
+        forward_expert(1)
+        forward_end(0)
+        give_back(1)
+        forward_end(1)
+        backward_send(0)
+        take_rows(2)
+        backward_send(1)
+        backward_expert(0)
+        give_back(2)
+        take_rows(3)
+        backward_expert(1)
+        give_back(3)
+        router_three()
+        backward_end(0)
+        backward_end(1)
+
+    @pl.when(section == 1)
+    def _():
+        forward_ready(0)
+        send_dispatch(0)
+        take_rows(0)
+        forward_ready(1)
+        send_dispatch(1)
+        forward_expert(0)
+        give_back(0)
+        take_rows(1)
+        forward_expert(1)
+        give_back(1)
+        forward_end(0)
+        backward_send(0)
+        forward_end(1)
+        backward_send(1)
+        take_rows(2)
+        backward_expert(0)
+        give_back(2)
+        take_rows(3)
+        backward_expert(1)
+        backward_end(0)
+        give_back(3)
+        router_three()
+        backward_end(1)
+
     wait_bytes(r3, r_recv.at[2])
     rgrad[...] = r3[...]
 
     for phase in range(4):
         wait_bytes(disp.at[phase, pl.ds(0, group - 1)], disp_send.at[phase])
-        wait_bytes(comb.at[phase, pl.ds(0, group - 1)], comb_send.at[phase])
+        wait_bytes(comb[phase].at[pl.ds(0, group - 1)], comb_send.at[phase])
         for g in range(n_group):
             wait_bytes(xb.at[phase, g, core], x_send.at[phase, g])
         wait_bytes(osend.at[phase], o_send.at[phase])
@@ -535,7 +579,10 @@
         pltpu.VMEM((4, n_out, rows, 256), bf),
         pltpu.VMEM((4, n_out, rows, 256), bf),
         pltpu.VMEM((4, group, cap) + block, bf),
-        pltpu.VMEM((4, group, cap) + block, bf),
+        pltpu.VMEM((group, cap) + block, bf),
+        pltpu.VMEM((group, cap) + block, bf),
+        pltpu.VMEM((group, cap) + block, bf),
+        pltpu.VMEM((group, cap) + block, bf),
         pltpu.VMEM((n_exp,) + block, f32),
         pltpu.VMEM((n_exp,) + block, f32),
         pltpu.VMEM((dp,) + block, f32),

time: 220 us -> 186 us (0.85)
  Pallas kernels: 207 us -> 174 us
    pallas_call x1, Pallas kernels: 207 us -> 174 us  [per_device(): pl.pallas_call(lambda *refs: relay_kernel(dims, *refs), out_shape=(jax.Sh...]
where the time goes in v2:
time: 186 us
  Pallas kernels  174 us (94%)
  local copies, waits for them, and re-layouts  7.85 us (4%)
  other arithmetic  3.1 us (2%)
    pallas_call x1, Pallas kernels, per_device(): pl.pallas_call(lambda *refs: relay_kernel(dims, *refs), out_shape=(jax.Sh...  174 us

profile of v2, /device:TPU:1, one launch (start us, length us, event | category | flops | bytes accessed | tf_op | source)
XLA Modules:
  0.0 185.6 jit_solution(3699320788431750542)
XLA Ops:
  0.7 0.8 copy.13
  1.4 0.1 reshape_squeeze.3
  1.5 0.2 convert_reduce_fusion
  1.7 0.1 select_reduce_fusion
  1.8 0.7 pad_add_fusion.refs_0_
  2.5 1.3 convert_element_type.18
  3.8 0.8 convert_bitcast_fusion
  4.6 0.7 copy.23
  5.3 1.6 copy_bitcast_fusion.1
  6.9 174.0 %relay.1 = (bf16[2,8,24,128]{3,2,1,0:T(8,128)(2,1)}, bf16[2,8,24,128]{3,2,1,0:T(8,128)(2,1)}, f32[8,24,128]{2,1,0:T(8,128)}) custom-call(s32[2,56]{1,0:T(2,128)} %pad_add_fusion.refs_0_, bf16[2,8,24,128]{3,2,1,0:T(8,128)(2,1)} %get-tuple-element.10.refs_1_, bf16[2,8,24,128]{3,2,1,0:T(8,128)(2,1)} %get-tuple-element.9.refs_2_, f32[24,128]{1,0:T(8,128)} %bitcast.46, ...), custom_call_target="tpu_custom_call" | custom-call | tf_op jit(solution)/shard_map/relay/pallas_call | solution.py:608
  180.9 1.6 reshape.65
  182.4 1.6 reshape.66
  184.0 1.6 copy.22
  (4 shorter events, 0.0 us)

commit v3 on v2

--- a/solution.py
+++ b/solution.py
@@ -6,6 +6,8 @@
 from jax.sharding import PartitionSpec as P
 
 EPSILON = 1e-05
+TILE_FF = 512
+TILE_OUT = 512
 MESH = pl.DeviceIdType.MESH
 NT = (((1,), (1,)), ((), ()))
 
@@ -24,12 +26,17 @@
     wg_hbm,
     wu_hbm,
     wd_hbm,
-    acts,
-    grads,
+    acts_out,
+    grads_out,
     rgrad,
     wg,
     wu,
     wd,
+    acts,
+    grads,
+    gain_f,
+    router_f,
+    flat,
     lin,
     ups,
     hid,
@@ -47,11 +54,16 @@
     obuf,
     osend,
     orecv,
-    snd2,
-    comb_0,
-    comb_1,
-    comb_2,
-    comb_3,
+    snd2_early,
+    snd2_late,
+    early_0,
+    early_1,
+    early_2,
+    early_3,
+    late_0,
+    late_1,
+    late_2,
+    late_3,
     racc,
     r1,
     r2,
@@ -71,13 +83,12 @@
     r_send,
     r_recv,
 ):
-    n_exp, n_x, cap, toks, chunks, n_ff, n_out, width = dims
+    n_exp, n_x, cap, toks, chunks, n_ff, n_out, n_early, n_batch, tile_ff, tile_out = dims
     group = n_exp * n_x
     rows = group * cap
     per_x = cap * chunks
     inv_count = 1.0 / (chunks * 128)
-    n_group, k_group = xb.shape[1], xb.shape[4]
-    group_chunks = k_group // 128
+    batch = group // n_batch
     none = 2 * toks
 
     section = lax.axis_index("section")
@@ -87,7 +98,10 @@
     core = lax.rem(my_dp, 2)
     me = my_e * n_x + my_x
 
-    comb = (comb_0, comb_1, comb_2, comb_3)
+    comb = ((early_0, late_0), (early_1, late_1), (early_2, late_2), (early_3, late_3))
+    snd2 = (snd2_early, snd2_late)
+    tile_chunks = tile_out // 128
+    starts, stops = (0, n_early), (n_early, n_out)
 
     def peer(step):
         q = lax.rem(me + step, group)
@@ -118,19 +132,40 @@
 
     pl.semaphore_signal(barrier, inc=1, device_id=partner, device_id_type=MESH)
 
+    def rows_to_blocks(source, target):
+        for m in range(2):
+            for j in range(chunks):
+                piece = source[m, :, j * 128 : (j + 1) * 128]
+                flat[j * toks : (j + 1) * toks, :] = piece.astype(jnp.float32)
+            for t in range(toks):
+                target[m, t] = flat[pl.ds(t, chunks, stride=toks), :].astype(jnp.bfloat16)
+
+    def blocks_to_rows(source, target, m):
+        for t in range(toks):
+            flat[pl.ds(t, chunks, stride=toks), :] = source[m, t].astype(jnp.float32)
+        for j in range(chunks):
+            piece = flat[j * toks : (j + 1) * toks, :]
+            target[m, :, j * 128 : (j + 1) * 128] = piece.astype(jnp.bfloat16)
+
     @pl.when(section == 0)
     def _():
-        lin[...] = x_in[...]
+        rows_to_blocks(x_in, lin)
 
     @pl.when(section == 1)
     def _():
-        ups[...] = cot_in[...]
+        rows_to_blocks(cot_in, ups)
+
+    for j in range(chunks):
+        gain_f[j : j + 1, :] = gain_in[0:1, j * 128 : (j + 1) * 128].astype(jnp.float32)
+    for j in range(chunks):
+        piece = router_in[:, j * 128 : (j + 1) * 128]
+        flat[j * n_exp : (j + 1) * n_exp, :] = piece.astype(jnp.float32)
+    for e in range(n_exp):
+        router_f[e] = flat[pl.ds(e, chunks, stride=n_exp), :]
 
     hid[:, toks] = jnp.zeros_like(hid[:, toks])
     scl[:, none] = jnp.zeros_like(scl[:, none])
-    pl.semaphore_wait(barrier, group + n_x)
-
-    gain = gain_in[...]
+    gain = gain_f[...]
 
     def total(v):
         return jnp.sum(v, axis=(0, 1), keepdims=True)
@@ -145,39 +180,52 @@
         return table[m, n_exp * cap + none + 2 * t + k]
 
     def router_diff(m, t):
-        return router_in[route(m, t, 0)] - router_in[route(m, t, 1)]
+        return router_f[route(m, t, 0)] - router_f[route(m, t, 1)]
+
+    def each_step(body):
+        for step in range(1, 4):
+            body(step)
+
+        @pl.loop(1, group // 4)
+        def _(turn):
+            for part in range(4):
+                body(turn * 4 + part)
 
     def send_dispatch(phase):
-        own = pltpu.make_async_copy(snd.at[phase, my_e], disp.at[phase, me], disp_recv.at[phase])
-        own.start()
-
-        @pl.loop(1, group)
-        def _(step):
+        pltpu.make_async_copy(
+            snd.at[phase, my_e], disp.at[phase, core, 0], disp_recv.at[phase, 0]
+        ).start()
+
+        def send(step):
             q, where = peer(step)
             pltpu.make_async_remote_copy(
                 src_ref=snd.at[phase, q // n_x],
-                dst_ref=disp.at[phase, me],
+                dst_ref=disp.at[phase, core, step],
                 send_sem=disp_send.at[phase],
-                recv_sem=disp_recv.at[phase],
+                recv_sem=disp_recv.at[phase, step // batch],
                 device_id=where,
                 device_id_type=MESH,
             ).start()
 
-    def send_combine(phase):
-        own = pltpu.make_async_copy(snd2.at[phase, me], comb[phase].at[me], comb_recv.at[phase])
-        own.start()
-
-        @pl.loop(1, group)
-        def _(step):
-            q, where = peer(step)
+        each_step(send)
+
+    def send_combine(phase, part):
+        pltpu.make_async_copy(
+            snd2[part].at[phase, 0], comb[phase][part].at[me], comb_recv.at[phase, part]
+        ).start()
+
+        def send(step):
+            _, where = peer(group - step)
             pltpu.make_async_remote_copy(
-                src_ref=snd2.at[phase, q],
-                dst_ref=comb[phase].at[me],
-                send_sem=comb_send.at[phase],
-                recv_sem=comb_recv.at[phase],
+                src_ref=snd2[part].at[phase, step],
+                dst_ref=comb[phase][part].at[me],
+                send_sem=comb_send.at[phase, part],
+                recv_sem=comb_recv.at[phase, part],
                 device_id=where,
                 device_id_type=MESH,
             ).start()
+
+        each_step(send)
 
     def hop(ref, dst, which, m):
         return pltpu.make_async_remote_copy(
@@ -189,59 +237,82 @@
             device_id_type=MESH,
         )
 
+    def batch_of(phase, half, b):
+        return disp.at[phase, half, pl.ds(b * batch, batch)]
+
+    def unpack(phase, half, b):
+        @pl.loop(b * batch, (b + 1) * batch)
+        def _(q):
+            block = disp[phase, half, q].astype(jnp.float32).reshape(per_x, 128)
+            xf[pl.ds(pl.multiple_of(q * per_x, 8), per_x), :] = block
+
+    def to_rows(half):
+        for j in range(chunks):
+            part = xf[pl.ds(j, rows, stride=chunks), :]
+            xb[half, :, j * 128 : (j + 1) * 128] = part.astype(jnp.bfloat16)
+
     def take_rows(phase):
-        wait_bytes(disp.at[phase], disp_recv.at[phase])
-
-        @pl.loop(0, group)
-        def _(q):
-            block = disp[phase, q].astype(jnp.float32).reshape(per_x, 128)
-            xf[pl.ds(pl.multiple_of(q * per_x, 8), per_x), :] = block
-
-        for g in range(n_group):
-            for i in range(group_chunks):
-                part = xf[pl.ds(g * group_chunks + i, rows, stride=chunks), :]
-                xb[phase, g, core, :, i * 128 : (i + 1) * 128] = part.astype(jnp.bfloat16)
+        for b in range(n_batch):
+            wait_bytes(batch_of(phase, core, b), disp_recv.at[phase, b])
             pltpu.make_async_remote_copy(
-                src_ref=xb.at[phase, g, core],
-                dst_ref=xb.at[phase, g, core],
-                send_sem=x_send.at[phase, g],
-                recv_sem=x_recv.at[phase, g],
+                src_ref=batch_of(phase, core, b),
+                dst_ref=batch_of(phase, core, b),
+                send_sem=x_send.at[phase],
+                recv_sem=x_recv.at[phase, b],
                 device_id=sibling,
                 device_id_type=MESH,
             ).start()
+            unpack(phase, core, b)
+        to_rows(core)
 
     def sibling_rows(phase):
-        for g in range(n_group):
-            wait_bytes(xb.at[phase, g, 1 - core], x_recv.at[phase, g])
-
-    def left(phase, g):
-        return xb[phase, g].reshape(2 * rows, k_group)
+        for b in range(n_batch):
+            wait_bytes(batch_of(phase, 1 - core, b), x_recv.at[phase, b])
+            unpack(phase, 1 - core, b)
+        to_rows(1 - core)
+
+    def left():
+        return xb[...].reshape(2 * rows, chunks * 128)
 
     def share_tile(phase, n, tile):
-        obuf[n] = tile.reshape(2, rows, 256)
+        obuf[n] = tile.reshape(2, rows, tile_out)
         osend[phase, n] = obuf[n, 1 - core].astype(jnp.bfloat16)
         pltpu.make_async_remote_copy(
             src_ref=osend.at[phase, n],
             dst_ref=orecv.at[phase, n],
             send_sem=o_send.at[phase],
-            recv_sem=o_recv.at[phase],
+            recv_sem=o_recv.at[phase, n // n_early],
             device_id=sibling,
             device_id_type=MESH,
         ).start()
 
-    def give_back(phase):
-        wait_bytes(orecv.at[phase], o_recv.at[phase])
-        for n in range(n_out):
+    def give_back(phase, part=1):
+        first, last = starts[part], stops[part]
+        span = (last - first) * tile_chunks
+        wait_bytes(orecv.at[phase, pl.ds(first, last - first)], o_recv.at[phase, part])
+        for n in range(first, last):
             both = obuf[n, core] + orecv[phase, n].astype(jnp.float32)
-            for i in range(2):
-                xf[pl.ds(2 * n + i, rows, stride=chunks), :] = both[:, i * 128 : (i + 1) * 128]
+            for i in range(tile_chunks):
+                at = (n - first) * tile_chunks + i
+                xf[pl.ds(at, rows, stride=span), :] = both[:, i * 128 : (i + 1) * 128]
 
         @pl.loop(0, group)
         def _(q):
-            block = xf[pl.ds(pl.multiple_of(q * per_x, 8), per_x), :]
-            snd2[phase, q] = block.reshape(cap, chunks, 128).astype(jnp.bfloat16)
-
-        send_combine(phase)
+            size = cap * span
+            block = xf[pl.ds(pl.multiple_of(q * size, 8), size), :]
+            snd2[part][phase, q] = block.reshape(cap, span, 128).astype(jnp.bfloat16)
+
+        send_combine(phase, part)
+
+    def over_tiles(phase, body):
+        pl.loop(0, min(n_early + 1, n_out))(body)
+        give_back(phase, 0)
+        if n_early + 1 < n_out:
+            pl.loop(n_early + 1, n_out)(body)
+
+    def await_combine(phase):
+        for part in range(2):
+            wait_bytes(comb[phase][part], comb_recv.at[phase, part])
 
     def fill_slots(phase, m, source, shift):
         for e in range(n_exp):
@@ -251,10 +322,13 @@
     def picked_of(phase, m, t, k):
         slot = table[m, n_exp * cap + 2 * t + k]
         e, s = slot // cap, lax.rem(slot, cap)
-        result = comb[phase][e * n_x, s].astype(jnp.float32)
-        for x in range(1, n_x):
-            result = result + comb[phase][e * n_x + x, s].astype(jnp.float32)
-        return result
+        parts = []
+        for ref in comb[phase]:
+            result = ref[e * n_x, s].astype(jnp.float32)
+            for x in range(1, n_x):
+                result = result + ref[e * n_x + x, s].astype(jnp.float32)
+            parts.append(result)
+        return jnp.concatenate(parts, axis=0)
 
     def forward_ready(m):
         @pl.when(section == 1)
@@ -278,33 +352,25 @@
 
         @pl.loop(0, n_ff)
         def _(n):
-            cols = pl.ds(pl.multiple_of(n * 256, 256), 256)
-            gate = jnp.zeros((2 * rows, 256), jnp.float32)
-            up = jnp.zeros((2 * rows, 256), jnp.float32)
-            for g in range(n_group):
-                x = left(m, g)
-                k = slice(g * k_group, (g + 1) * k_group)
-                gate = gate + jnp.dot(x, wg[k, cols], preferred_element_type=jnp.float32)
-                up = up + jnp.dot(x, wu[k, cols], preferred_element_type=jnp.float32)
+            cols = pl.ds(pl.multiple_of(n * tile_ff, tile_ff), tile_ff)
+            gate = jnp.dot(left(), wg[:, cols], preferred_element_type=jnp.float32)
             gs[m, n] = gate
+            up = jnp.dot(left(), wu[:, cols], preferred_element_type=jnp.float32)
             us[m, n] = up
-            act[n] = (gate * sigmoid(gate) * up).astype(jnp.bfloat16)
+            act[:, cols] = (gate * sigmoid(gate) * up).astype(jnp.bfloat16)
 
         if m == 0:
             weights[2].wait()
 
-        @pl.loop(0, n_out)
-        def _(n):
-            cols = pl.ds(pl.multiple_of(n * 256, 256), 256)
-            tile = jnp.zeros((2 * rows, 256), jnp.float32)
-            for k in range(n_ff):
-                tile = tile + jnp.dot(
-                    act[k], wd[k * 256 : (k + 1) * 256, cols], preferred_element_type=jnp.float32
-                )
+        def out_tile(n):
+            cols = pl.ds(pl.multiple_of(n * tile_out, tile_out), tile_out)
+            tile = jnp.dot(act[...], wd[:, cols], preferred_element_type=jnp.float32)
             share_tile(m, n, tile)
 
+        over_tiles(m, out_tile)
+
     def forward_end(m):
-        wait_bytes(comb[m], comb_recv.at[m])
+        await_combine(m)
         for t in range(toks):
             p0 = prob[m, t, 0, 0:1, 0:1]
             p1 = prob[m, t, 1, 0:1, 0:1]
@@ -316,6 +382,8 @@
         @pl.when(section == 0)
         def _():
             hop(acts, lin, 0, m).start()
+
+        blocks_to_rows(acts, acts_out, m)
 
     def backward_send(m):
         phase = 2 + m
@@ -402,40 +470,31 @@
 
         @pl.loop(0, n_ff)
         def _(n):
-            part = pl.ds(pl.multiple_of(n * 256, 256), 256)
-            d_act = jnp.zeros((2 * rows, 256), jnp.float32)
-            for g in range(n_group):
-                d_act = d_act + lax.dot_general(
-                    left(phase, g),
-                    wd[part, g * k_group : (g + 1) * k_group],
-                    NT,
-                    preferred_element_type=jnp.float32,
-                )
+            part = pl.ds(pl.multiple_of(n * tile_ff, tile_ff), tile_ff)
+            d_act = lax.dot_general(
+                left(), wd[part, :], NT, preferred_element_type=jnp.float32
+            )
             gate, up = gs[m, n], us[m, n]
             sig = sigmoid(gate)
-            act[n] = (d_act * up * sig * (1.0 + gate * (1.0 - sig))).astype(jnp.bfloat16)
-            act2[n] = (d_act * gate * sig).astype(jnp.bfloat16)
+            act[:, part] = (d_act * up * sig * (1.0 + gate * (1.0 - sig))).astype(jnp.bfloat16)
+            act2[:, part] = (d_act * gate * sig).astype(jnp.bfloat16)
 
         if m:
             router_two()
 
-        @pl.loop(0, n_out)
-        def _(n):
-            part = pl.ds(pl.multiple_of(n * 256, 256), 256)
-            tile = jnp.zeros((2 * rows, 256), jnp.float32)
-            for k in range(n_ff):
-                cols = slice(k * 256, (k + 1) * 256)
-                tile = tile + lax.dot_general(
-                    act[k], wg[part, cols], NT, preferred_element_type=jnp.float32
-                )
-                tile = tile + lax.dot_general(
-                    act2[k], wu[part, cols], NT, preferred_element_type=jnp.float32
-                )
+        def back_tile(n):
+            part = pl.ds(pl.multiple_of(n * tile_out, tile_out), tile_out)
+            tile = lax.dot_general(act[...], wg[part, :], NT, preferred_element_type=jnp.float32)
+            tile = tile + lax.dot_general(
+                act2[...], wu[part, :], NT, preferred_element_type=jnp.float32
+            )
             share_tile(phase, n, tile)
+
+        over_tiles(phase, back_tile)
 
     def backward_end(m):
         phase = 2 + m
-        wait_bytes(comb[phase], comb_recv.at[phase])
+        await_combine(phase)
         for t in range(toks):
             d_gap = prob[m, t, 2, 0:1, 0:1]
             d_hidden = picked_of(phase, m, t, 0) + picked_of(phase, m, t, 1)
@@ -452,9 +511,16 @@
         def _():
             hop(grads, ups, 1, m).start()
 
+        blocks_to_rows(grads, grads_out, m)
+
     @pl.when(section == 0)
     def _():
         forward_ready(0)
+
+    pl.semaphore_wait(barrier, group + n_x)
+
+    @pl.when(section == 0)
+    def _():
         send_dispatch(0)
         forward_ready(1)
         take_rows(0)
@@ -505,13 +571,17 @@
         backward_end(1)
 
     wait_bytes(r3, r_recv.at[2])
-    rgrad[...] = r3[...]
+    for e in range(n_exp):
+        flat[pl.ds(e, chunks, stride=n_exp), :] = r3[e]
+    for j in range(chunks):
+        rgrad[:, j * 128 : (j + 1) * 128] = flat[j * n_exp : (j + 1) * n_exp, :]
 
     for phase in range(4):
-        wait_bytes(disp.at[phase, pl.ds(0, group - 1)], disp_send.at[phase])
-        wait_bytes(comb[phase].at[pl.ds(0, group - 1)], comb_send.at[phase])
-        for g in range(n_group):
-            wait_bytes(xb.at[phase, g, core], x_send.at[phase, g])
+        wait_bytes(disp.at[phase, core, pl.ds(0, group - 1)], disp_send.at[phase])
+        for part in range(2):
+            sent = comb[phase][part].at[pl.ds(0, group - 1)]
+            wait_bytes(sent, comb_send.at[phase, part])
+        wait_bytes(disp.at[phase, core], x_send.at[phase])
         wait_bytes(osend.at[phase], o_send.at[phase])
     wait_bytes(r1.at[pl.ds(0, n_exp - 1)], r_send.at[0])
     wait_bytes(r2.at[pl.ds(0, 2 * n_x - 1)], r_send.at[1])
@@ -525,6 +595,12 @@
         @pl.when(section == 1)
         def _():
             hop(grads, ups, 1, m).wait_send()
+
+
+def finish_kernel(acts, grads, rgrad, acts_out, grads_out, rgrad_out):
+    acts_out[...] = acts[...]
+    grads_out[...] = grads[...]
+    rgrad_out[...] = rgrad[...]
 
 
 def slot_tables(picks, cap, experts):
@@ -548,14 +624,17 @@
     cap = 3
     chunks = width // 128
     hidden_units = w_gate.shape[3]
-    n_ff, n_out = hidden_units // 256, width // 256
+    tile_ff, tile_out = min(TILE_FF, hidden_units), min(TILE_OUT, width)
+    n_ff, n_out = hidden_units // tile_ff, width // tile_out
     group = n_exp * n_x
     rows = group * cap
-    n_group = 4
-    k_group = width // n_group
+    n_batch = 4
     table = slot_tables(routes[0], cap, experts)
     bf, f32 = jnp.bfloat16, jnp.float32
     block = (chunks, 128)
+    n_early = max(n_out * 2 // 3, 1)
+    early = (n_early * tile_out // 128, 128)
+    late = ((n_out - n_early) * tile_out // 128, 128)
     dma = pltpu.SemaphoreType.DMA
     scratch = [
         pltpu.VMEM((width, hidden_units), bf),
@@ -563,26 +642,36 @@
         pltpu.VMEM((hidden_units, width), bf),
         pltpu.VMEM((micro, toks) + block, bf),
         pltpu.VMEM((micro, toks) + block, bf),
+        pltpu.VMEM(block, f32),
+        pltpu.VMEM((experts,) + block, f32),
+        pltpu.VMEM((chunks * 8, 128), f32),
+        pltpu.VMEM((micro, toks) + block, bf),
+        pltpu.VMEM((micro, toks) + block, bf),
         pltpu.VMEM((micro, toks + 1) + block, bf),
         pltpu.VMEM((micro, 2 * toks + 1) + block, bf),
         pltpu.VMEM((micro, toks, 3, 8, 128), f32),
         pltpu.VMEM((micro, toks) + block, f32),
         pltpu.VMEM((4, n_exp, cap) + block, bf),
-        pltpu.VMEM((4, group, cap) + block, bf),
+        pltpu.VMEM((4, 2, group, cap) + block, bf),
         pltpu.VMEM((rows * chunks, 128), f32),
-        pltpu.VMEM((4, n_group, 2, rows, k_group), bf),
-        pltpu.VMEM((micro, n_ff, 2 * rows, 256), f32),
-        pltpu.VMEM((micro, n_ff, 2 * rows, 256), f32),
-        pltpu.VMEM((n_ff, 2 * rows, 256), bf),
-        pltpu.VMEM((n_ff, 2 * rows, 256), bf),
-        pltpu.VMEM((n_out, 2, rows, 256), f32),
-        pltpu.VMEM((4, n_out, rows, 256), bf),
-        pltpu.VMEM((4, n_out, rows, 256), bf),
-        pltpu.VMEM((4, group, cap) + block, bf),
-        pltpu.VMEM((group, cap) + block, bf),
-        pltpu.VMEM((group, cap) + block, bf),
-        pltpu.VMEM((group, cap) + block, bf),
-        pltpu.VMEM((group, cap) + block, bf),
+        pltpu.VMEM((2, rows, width), bf),
+        pltpu.VMEM((micro, n_ff, 2 * rows, tile_ff), f32),
+        pltpu.VMEM((micro, n_ff, 2 * rows, tile_ff), f32),
+        pltpu.VMEM((2 * rows, hidden_units), bf),
+        pltpu.VMEM((2 * rows, hidden_units), bf),
+        pltpu.VMEM((n_out, 2, rows, tile_out), f32),
+        pltpu.VMEM((4, n_out, rows, tile_out), bf),
+        pltpu.VMEM((4, n_out, rows, tile_out), bf),
+        pltpu.VMEM((4, group, cap) + early, bf),
+        pltpu.VMEM((4, group, cap) + late, bf),
+        pltpu.VMEM((group, cap) + early, bf),
+        pltpu.VMEM((group, cap) + early, bf),
+        pltpu.VMEM((group, cap) + early, bf),
+        pltpu.VMEM((group, cap) + early, bf),
+        pltpu.VMEM((group, cap) + late, bf),
+        pltpu.VMEM((group, cap) + late, bf),
+        pltpu.VMEM((group, cap) + late, bf),
+        pltpu.VMEM((group, cap) + late, bf),
         pltpu.VMEM((n_exp,) + block, f32),
         pltpu.VMEM((n_exp,) + block, f32),
         pltpu.VMEM((dp,) + block, f32),
@@ -590,27 +679,27 @@
         pltpu.VMEM((2,) + block, f32),
         dma((3,)),
         dma((4,)),
+        dma((4, n_batch)),
         dma((4,)),
-        dma((4, n_group)),
-        dma((4, n_group)),
+        dma((4, n_batch)),
         dma((4,)),
-        dma((4,)),
-        dma((4,)),
-        dma((4,)),
+        dma((4, 2)),
+        dma((4, 2)),
+        dma((4, 2)),
         dma((2, micro)),
         dma((2, micro)),
         dma((3,)),
         dma((3,)),
     ]
-    dims = (n_exp, n_x, cap, toks, chunks, n_ff, n_out, width)
+    dims = (n_exp, n_x, cap, toks, chunks, n_ff, n_out, n_early, n_batch, tile_ff, tile_out)
     vmem = pl.BlockSpec(memory_space=pltpu.VMEM)
     hbm = pl.BlockSpec(memory_space=pl.ANY)
     acts, grads, rgrad = pl.pallas_call(
         lambda *refs: relay_kernel(dims, *refs),
         out_shape=(
-            jax.ShapeDtypeStruct((micro, toks) + block, bf),
-            jax.ShapeDtypeStruct((micro, toks) + block, bf),
-            jax.ShapeDtypeStruct((experts,) + block, f32),
+            jax.ShapeDtypeStruct((micro, toks, width), bf),
+            jax.ShapeDtypeStruct((micro, toks, width), bf),
+            jax.ShapeDtypeStruct((experts, width), f32),
         ),
         in_specs=[pl.BlockSpec(memory_space=pltpu.SMEM)] + [vmem] * 4 + [hbm] * 3,
         out_specs=(vmem, vmem, vmem),
@@ -621,18 +710,25 @@
         name="relay",
     )(
         table,
-        inputs.reshape((micro, toks) + block),
-        cotangent.reshape((micro, toks) + block),
-        norm_gain[0].astype(f32).reshape(block),
-        router[0].astype(f32).T.reshape((experts,) + block),
+        inputs,
+        cotangent,
+        norm_gain,
+        router[0].T,
         w_gate[0, 0],
         w_up[0, 0],
         w_down[0, 0],
     )
+    acts, grads, rgrad = pl.pallas_call(
+        finish_kernel,
+        out_shape=tuple(jax.ShapeDtypeStruct(a.shape, a.dtype) for a in (acts, grads, rgrad)),
+        in_specs=[vmem] * 3,
+        out_specs=(vmem,) * 3,
+        name="finish",
+    )(acts, grads, rgrad)
     return (
-        acts.reshape(1, micro, toks, width),
-        grads.reshape(1, micro, toks, width),
-        rgrad.reshape(experts, width).T[None],
+        acts[None],
+        grads[None],
+        rgrad.T[None],
     )
 
 

time: 186 us -> 179 us (0.962)
  local copies, waits for them, and re-layouts: 7.85 us -> 0.85 us
  Pallas kernels: 174 us -> 177 us
  other arithmetic: 3.1 us -> 0.95 us
    reshape x3 -> x0, local copies, waits for them, and re-layouts: 4.8 us -> none  [the longest x1 1.64 us: per_device(): cotangent.reshape((micro, toks) + block)]
    unnamed x3 -> x1, local copies, waits for them, and re-layouts: 2.97 us -> 0.76 us
where the time goes in v3:
time: 179 us
  Pallas kernels  177 us (99%)
    pallas_call x1, Pallas kernels, per_device(): pl.pallas_call(lambda *refs: relay_kernel(dims, *refs), out_shape=(jax.Sh...  175 us

profile of v3, /device:TPU:1, one launch (start us, length us, event | category | flops | bytes accessed | tf_op | source)
XLA Modules:
  0.0 179.1 jit_solution(3953832160864885069)
XLA Ops:
  0.7 0.8 copy.13
  1.4 0.1 reshape_squeeze.3
  1.5 0.2 convert_reduce_fusion
  1.7 0.1 select_reduce_fusion
  1.8 0.6 pad_add_fusion.refs_0_
  2.4 174.9 %relay.1 = (bf16[2,8,3072]{2,1,0:T(8,128)(2,1)}, bf16[2,8,3072]{2,1,0:T(8,128)(2,1)}, f32[8,3072]{1,0:T(8,128)}) custom-call(s32[2,56]{1,0:T(2,128)} %pad_add_fusion.refs_0_, bf16[2,8,3072]{2,1,0:T(8,128)(2,1)} %refs_1_.1, bf16[2,8,3072]{2,1,0:T(8,128)(2,1)} %refs_2_.1, bf16[1,3072]{1,0:T(2,128)(2,1)} %refs_3_.1, bf16[8,3072]{1,0:T(8,128)(2,1)} %bitcast.16, ...), custom_call_target="tpu_custom_call" | custom-call | tf_op jit(solution)/shard_map/relay/pallas_call | solution.py:697
  177.4 1.7 finish.1
  (4 shorter events, 0.0 us)

commit v4 on v3

--- a/solution.py
+++ b/solution.py
@@ -54,16 +54,11 @@
     obuf,
     osend,
     orecv,
-    snd2_early,
-    snd2_late,
-    early_0,
-    early_1,
-    early_2,
-    early_3,
-    late_0,
-    late_1,
-    late_2,
-    late_3,
+    snd2,
+    comb_0,
+    comb_1,
+    comb_2,
+    comb_3,
     racc,
     r1,
     r2,
@@ -98,14 +93,32 @@
     core = lax.rem(my_dp, 2)
     me = my_e * n_x + my_x
 
-    comb = ((early_0, late_0), (early_1, late_1), (early_2, late_2), (early_3, late_3))
-    snd2 = (snd2_early, snd2_late)
+    comb = (comb_0, comb_1, comb_2, comb_3)
     tile_chunks = tile_out // 128
-    starts, stops = (0, n_early), (n_early, n_out)
-
-    def peer(step):
-        q = lax.rem(me + step, group)
-        return q, {"expert": q // n_x, "dp": lax.rem(q, n_x) * 2 + core}
+    halves = ((0, n_early), (n_early, n_out))
+
+    def pieces_of(phase):
+        return ((0, n_out),) if phase < 2 else halves
+
+    def span_of(piece):
+        return pl.ds(piece[0] * tile_chunks, (piece[1] - piece[0]) * tile_chunks)
+
+    def wrapped(value, size):
+        return jnp.where(value >= size, value - size, value)
+
+    ahead = [wrapped(my_x + dx, n_x) * 2 + core for dx in range(n_x)]
+    behind = [wrapped(my_x + n_x - dx, n_x) * 2 + core for dx in range(n_x)]
+
+    def each_step(body, back=False):
+        columns = behind if back else ahead
+        for dx in range(1, n_x):
+            body(0, dx, my_e, {"expert": my_e, "dp": columns[dx]})
+
+        @pl.loop(1, n_exp)
+        def _(de):
+            e = wrapped(my_e + n_exp - de if back else my_e + de, n_exp)
+            for dx in range(n_x):
+                body(de, dx, e, {"expert": e, "dp": columns[dx]})
 
     sibling = {"dp": my_x * 2 + 1 - core}
     partner = {"section": 1 - section}
@@ -119,10 +132,10 @@
 
     barrier = pltpu.get_barrier_semaphore()
 
-    @pl.loop(1, group)
-    def _(step):
-        _, where = peer(step)
+    def greet(de, dx, e, where):
         pl.semaphore_signal(barrier, inc=1, device_id=where, device_id_type=MESH)
+
+    each_step(greet)
 
     @pl.loop(0, n_x)
     def _(x):
@@ -182,27 +195,17 @@
     def router_diff(m, t):
         return router_f[route(m, t, 0)] - router_f[route(m, t, 1)]
 
-    def each_step(body):
-        for step in range(1, 4):
-            body(step)
-
-        @pl.loop(1, group // 4)
-        def _(turn):
-            for part in range(4):
-                body(turn * 4 + part)
-
     def send_dispatch(phase):
         pltpu.make_async_copy(
             snd.at[phase, my_e], disp.at[phase, core, 0], disp_recv.at[phase, 0]
         ).start()
 
-        def send(step):
-            q, where = peer(step)
+        def send(de, dx, e, where):
             pltpu.make_async_remote_copy(
-                src_ref=snd.at[phase, q // n_x],
-                dst_ref=disp.at[phase, core, step],
+                src_ref=snd.at[phase, e],
+                dst_ref=disp.at[phase, core, de * n_x + dx],
                 send_sem=disp_send.at[phase],
-                recv_sem=disp_recv.at[phase, step // batch],
+                recv_sem=disp_recv.at[phase, de // (batch // n_x)],
                 device_id=where,
                 device_id_type=MESH,
             ).start()
@@ -210,22 +213,22 @@
         each_step(send)
 
     def send_combine(phase, part):
+        span = span_of(pieces_of(phase)[part])
         pltpu.make_async_copy(
-            snd2[part].at[phase, 0], comb[phase][part].at[me], comb_recv.at[phase, part]
+            snd2.at[phase, 0, :, span], comb[phase].at[me, :, span], comb_recv.at[phase, part]
         ).start()
 
-        def send(step):
-            _, where = peer(group - step)
+        def send(de, dx, e, where):
             pltpu.make_async_remote_copy(
-                src_ref=snd2[part].at[phase, step],
-                dst_ref=comb[phase][part].at[me],
+                src_ref=snd2.at[phase, de * n_x + dx, :, span],
+                dst_ref=comb[phase].at[me, :, span],
                 send_sem=comb_send.at[phase, part],
                 recv_sem=comb_recv.at[phase, part],
                 device_id=where,
                 device_id_type=MESH,
             ).start()
 
-        each_step(send)
+        each_step(send, back=True)
 
     def hop(ref, dst, which, m):
         return pltpu.make_async_remote_copy(
@@ -286,10 +289,12 @@
             device_id_type=MESH,
         ).start()
 
-    def give_back(phase, part=1):
-        first, last = starts[part], stops[part]
+    def give_back(phase, part):
+        first, last = pieces_of(phase)[part]
         span = (last - first) * tile_chunks
-        wait_bytes(orecv.at[phase, pl.ds(first, last - first)], o_recv.at[phase, part])
+        for half, (low, high) in enumerate(halves):
+            if first <= low and high <= last:
+                wait_bytes(orecv.at[phase, pl.ds(low, high - low)], o_recv.at[phase, half])
         for n in range(first, last):
             both = obuf[n, core] + orecv[phase, n].astype(jnp.float32)
             for i in range(tile_chunks):
@@ -299,20 +304,22 @@
         @pl.loop(0, group)
         def _(q):
             size = cap * span
-            block = xf[pl.ds(pl.multiple_of(q * size, 8), size), :]
-            snd2[part][phase, q] = block.reshape(cap, span, 128).astype(jnp.bfloat16)
+            block = xf[pl.ds(pl.multiple_of(q * size, 8), size), :].reshape(cap, span, 128)
+            snd2[phase, q, :, span_of((first, last))] = block.astype(jnp.bfloat16)
 
         send_combine(phase, part)
 
     def over_tiles(phase, body):
-        pl.loop(0, min(n_early + 1, n_out))(body)
-        give_back(phase, 0)
-        if n_early + 1 < n_out:
-            pl.loop(n_early + 1, n_out)(body)
+        stop = min(n_early + 1, n_out) if phase > 1 else n_out
+        pl.loop(0, stop)(body)
+        if phase > 1:
+            give_back(phase, 0)
+        if stop < n_out:
+            pl.loop(stop, n_out)(body)
 
     def await_combine(phase):
-        for part in range(2):
-            wait_bytes(comb[phase][part], comb_recv.at[phase, part])
+        for part, piece in enumerate(pieces_of(phase)):
+            wait_bytes(comb[phase].at[:, :, span_of(piece)], comb_recv.at[phase, part])
 
     def fill_slots(phase, m, source, shift):
         for e in range(n_exp):
@@ -322,13 +329,10 @@
     def picked_of(phase, m, t, k):
         slot = table[m, n_exp * cap + 2 * t + k]
         e, s = slot // cap, lax.rem(slot, cap)
-        parts = []
-        for ref in comb[phase]:
-            result = ref[e * n_x, s].astype(jnp.float32)
-            for x in range(1, n_x):
-                result = result + ref[e * n_x + x, s].astype(jnp.float32)
-            parts.append(result)
-        return jnp.concatenate(parts, axis=0)
+        result = comb[phase][e * n_x, s].astype(jnp.float32)
+        for x in range(1, n_x):
+            result = result + comb[phase][e * n_x + x, s].astype(jnp.float32)
+        return result
 
     def forward_ready(m):
         @pl.when(section == 1)
@@ -526,20 +530,20 @@
         take_rows(0)
         send_dispatch(1)
         forward_expert(0)
-        give_back(0)
+        give_back(0, 0)
         take_rows(1)
         forward_expert(1)
         forward_end(0)
-        give_back(1)
+        give_back(1, 0)
         forward_end(1)
         backward_send(0)
+        backward_send(1)
         take_rows(2)
-        backward_send(1)
         backward_expert(0)
-        give_back(2)
+        give_back(2, 1)
         take_rows(3)
         backward_expert(1)
-        give_back(3)
+        give_back(3, 1)
         router_three()
         backward_end(0)
         backward_end(1)
@@ -548,25 +552,25 @@
     def _():
         forward_ready(0)
         send_dispatch(0)
-        take_rows(0)
         forward_ready(1)
         send_dispatch(1)
+        take_rows(0)
         forward_expert(0)
-        give_back(0)
+        give_back(0, 0)
         take_rows(1)
         forward_expert(1)
-        give_back(1)
+        give_back(1, 0)
         forward_end(0)
         backward_send(0)
         forward_end(1)
         backward_send(1)
         take_rows(2)
         backward_expert(0)
-        give_back(2)
+        give_back(2, 1)
         take_rows(3)
         backward_expert(1)
         backward_end(0)
-        give_back(3)
+        give_back(3, 1)
         router_three()
         backward_end(1)
 
@@ -578,8 +582,8 @@
 
     for phase in range(4):
         wait_bytes(disp.at[phase, core, pl.ds(0, group - 1)], disp_send.at[phase])
-        for part in range(2):
-            sent = comb[phase][part].at[pl.ds(0, group - 1)]
+        for part, piece in enumerate(pieces_of(phase)):
+            sent = comb[phase].at[pl.ds(0, group - 1), :, span_of(piece)]
             wait_bytes(sent, comb_send.at[phase, part])
         wait_bytes(disp.at[phase, core], x_send.at[phase])
         wait_bytes(osend.at[phase], o_send.at[phase])
@@ -628,13 +632,11 @@
     n_ff, n_out = hidden_units // tile_ff, width // tile_out
     group = n_exp * n_x
     rows = group * cap
-    n_batch = 4
+    n_batch = min(4, n_exp)
     table = slot_tables(routes[0], cap, experts)
     bf, f32 = jnp.bfloat16, jnp.float32
     block = (chunks, 128)
     n_early = max(n_out * 2 // 3, 1)
-    early = (n_early * tile_out // 128, 128)
-    late = ((n_out - n_early) * tile_out // 128, 128)
     dma = pltpu.SemaphoreType.DMA
     scratch = [
         pltpu.VMEM((width, hidden_units), bf),
@@ -662,16 +664,11 @@
         pltpu.VMEM((n_out, 2, rows, tile_out), f32),
         pltpu.VMEM((4, n_out, rows, tile_out), bf),
         pltpu.VMEM((4, n_out, rows, tile_out), bf),
-        pltpu.VMEM((4, group, cap) + early, bf),
-        pltpu.VMEM((4, group, cap) + late, bf),
-        pltpu.VMEM((group, cap) + early, bf),
-        pltpu.VMEM((group, cap) + early, bf),
-        pltpu.VMEM((group, cap) + early, bf),
-        pltpu.VMEM((group, cap) + early, bf),
-        pltpu.VMEM((group, cap) + late, bf),
-        pltpu.VMEM((group, cap) + late, bf),
-        pltpu.VMEM((group, cap) + late, bf),
-        pltpu.VMEM((group, cap) + late, bf),
+        pltpu.VMEM((4, group, cap) + block, bf),
+        pltpu.VMEM((group, cap) + block, bf),
+        pltpu.VMEM((group, cap) + block, bf),
+        pltpu.VMEM((group, cap) + block, bf),
+        pltpu.VMEM((group, cap) + block, bf),
         pltpu.VMEM((n_exp,) + block, f32),
         pltpu.VMEM((n_exp,) + block, f32),
         pltpu.VMEM((dp,) + block, f32),

time: 179 us -> 173 us (0.966)
  Pallas kernels: 177 us -> 170 us
    pallas_call x1, Pallas kernels: 175 us -> 169 us  [per_device(): pl.pallas_call(lambda *refs: relay_kernel(dims, *refs), out_shape=(jax.Sh...]
where the time goes in v4:
time: 173 us
  Pallas kernels  170 us (98%)
    pallas_call x1, Pallas kernels, per_device(): pl.pallas_call(lambda *refs: relay_kernel(dims, *refs), out_shape=(jax.Sh...  169 us

profile of v4, /device:TPU:1, one launch (start us, length us, event | category | flops | bytes accessed | tf_op | source)
XLA Modules:
  0.0 172.8 jit_solution(3801702508124027293)
XLA Ops:
  0.7 0.8 copy.13
  1.4 0.1 reshape_squeeze.3
  1.5 0.2 convert_reduce_fusion
  1.7 0.1 select_reduce_fusion
  1.8 0.6 pad_add_fusion.refs_0_
  2.4 168.6 %relay.1 = (bf16[2,8,3072]{2,1,0:T(8,128)(2,1)}, bf16[2,8,3072]{2,1,0:T(8,128)(2,1)}, f32[8,3072]{1,0:T(8,128)}) custom-call(s32[2,56]{1,0:T(2,128)} %pad_add_fusion.refs_0_, bf16[2,8,3072]{2,1,0:T(8,128)(2,1)} %refs_1_.1, bf16[2,8,3072]{2,1,0:T(8,128)(2,1)} %refs_2_.1, bf16[1,3072]{1,0:T(2,128)(2,1)} %refs_3_.1, bf16[8,3072]{1,0:T(8,128)(2,1)} %bitcast.16, ...), custom_call_target="tpu_custom_call" | custom-call | tf_op jit(solution)/shard_map/relay/pallas_call | solution.py:694
  171.0 1.7 finish.1
  (4 shorter events, 0.0 us)

commit v5 on v4

--- a/solution.py
+++ b/solution.py
@@ -309,9 +309,11 @@
 
         send_combine(phase, part)
 
-    def over_tiles(phase, body):
+    def over_tiles(phase, body, between=None):
         stop = min(n_early + 1, n_out) if phase > 1 else n_out
         pl.loop(0, stop)(body)
+        if between is not None:
+            between()
         if phase > 1:
             give_back(phase, 0)
         if stop < n_out:
@@ -468,7 +470,7 @@
                 device_id_type=MESH,
             ).start()
 
-    def backward_expert(m):
+    def backward_expert(m, between=None):
         phase = 2 + m
         sibling_rows(phase)
 
@@ -494,7 +496,7 @@
             )
             share_tile(phase, n, tile)
 
-        over_tiles(phase, back_tile)
+        over_tiles(phase, back_tile, between)
 
     def backward_end(m):
         phase = 2 + m
@@ -568,8 +570,7 @@
         backward_expert(0)
         give_back(2, 1)
         take_rows(3)
-        backward_expert(1)
-        backward_end(0)
+        backward_expert(1, lambda: backward_end(0))
         give_back(3, 1)
         router_three()
         backward_end(1)

time: 173 us -> 173 us (level)
  no operation moved by 1% of the time
where the time goes in v5:
time: 173 us
  Pallas kernels  170 us (98%)
    pallas_call x1, Pallas kernels, per_device(): pl.pallas_call(lambda *refs: relay_kernel(dims, *refs), out_shape=(jax.Sh...  169 us

profile of v5, /device:TPU:1, one launch (start us, length us, event | category | flops | bytes accessed | tf_op | source)
XLA Modules:
  0.0 172.8 jit_solution(7951865948935868936)
XLA Ops:
  0.7 0.8 copy.13
  1.4 0.1 reshape_squeeze.3
  1.5 0.2 convert_reduce_fusion
  1.7 0.1 select_reduce_fusion
  1.8 0.6 pad_add_fusion.refs_0_
  2.4 168.7 %relay.1 = (bf16[2,8,3072]{2,1,0:T(8,128)(2,1)}, bf16[2,8,3072]{2,1,0:T(8,128)(2,1)}, f32[8,3072]{1,0:T(8,128)}) custom-call(s32[2,56]{1,0:T(2,128)} %pad_add_fusion.refs_0_, bf16[2,8,3072]{2,1,0:T(8,128)(2,1)} %refs_1_.1, bf16[2,8,3072]{2,1,0:T(8,128)(2,1)} %refs_2_.1, bf16[1,3072]{1,0:T(2,128)(2,1)} %refs_3_.1, bf16[8,3072]{1,0:T(8,128)(2,1)} %bitcast.16, ...), custom_call_target="tpu_custom_call" | custom-call | tf_op jit(solution)/shard_map/relay/pallas_call | solution.py:695
  171.1 1.7 finish.1
  (4 shorter events, 0.0 us)
